TPU v7x, 512 devices: a whole 4x4x16 slice. The times are simulated.
512 devices in a mesh: mem: 8 (over x, core), gx: 4 (over z_hi), gy: 16 (over z_lo, y).
Axes of the slice: x: 4, y: 4, z: 16 (z_hi: 4, z_lo: 4; z = z_hi * 4 + z_lo), core: 2. Of those that a mesh axis runs over, the one named last changes fastest.
Arguments:
- control: float32 [64, 3, 512, 512], P('mem', None, 'gy', 'gx'), may hold values from -6 to 6
- perturb: bfloat16 [64, 6, 3, 512, 512], P('mem', None, None, 'gy', 'gx'), may hold values from -6 to 6
- obs_count: int32 [3, 512, 512], P(None, 'gy', 'gx'), may hold values from 0 to 3
- obs_weight: float32 [6], replicated, may hold values from 0.3 to 3
- diffusivity: float32 [3, 512, 512], P(None, 'gy', 'gx'), may hold values from 0.12 to 0.24
Outputs:
- hess_product: float32 [64, 3, 512, 512], P('mem', None, 'gy', 'gx')
All inputs are finite; a program needn't handle non-finite values.
Results may differ from a plain program's by a relative error of at most 0.0003.
Values sent between devices are 32-bit elements; how exact they have to be, the bound alone decides.
No kernel may reach another device: no remote copies, remote signals or barrier semaphores. Data moves between devices by JAX's collectives and lax.ppermute only.
A program may use at most 64 MiB of HBM per device.

v0:
```python
import math

import jax
import jax.numpy as jnp
from jax import lax
from jax.sharding import PartitionSpec as P

STEPS = 4


def padded_2(array, sides, width):
    for axis, dim in sides:
        size, length = (lax.axis_size(axis), array.shape[dim])
        up = [(i, (i + 1) % size) for i in range(size - 1)]
        down = [(j, i) for i, j in up]
        last = lax.slice_in_dim(array, length - width, length, axis=dim)
        initial = lax.slice_in_dim(array, 0, width, axis=dim)
        before = lax.ppermute(last, axis, up)
        after = lax.ppermute(initial, axis, down)
        array = jnp.concatenate([before, array, after], axis=dim)
    return array


def laplace(padded):
    return (
        padded[..., 2:, 1:-1]
        + padded[..., :-2, 1:-1]
        + padded[..., 1:-1, 2:]
        + padded[..., 1:-1, :-2]
        - 4.0 * padded[..., 1:-1, 1:-1]
    )


def forward_rim(field):
    return padded_2(field, (("gx", 3), ("gy", 2)), 1)


def backward_rim(field):
    return padded_2(field, (("gx", 3), ("gy", 2)), 1)


def shards(control, perturb, obs_count, obs_weight, diffusivity):
    members_all = control.shape[0] * lax.axis_size("mem")
    ensemble_scale = 1.0 / math.sqrt(members_all - 1)
    spread = control
    for step_index in range(STEPS):
        spread = spread + diffusivity * laplace(forward_rim(spread))
    member_terms = jnp.sum(perturb.astype(jnp.float32) * spread[:, None], axis=0) * ensemble_scale
    var_weight = obs_weight[:, None, None, None]
    increment = lax.psum(member_terms, "mem")
    weighted = obs_count.astype(jnp.float32)[None] * var_weight * increment
    back = jnp.sum(perturb.astype(jnp.float32) * weighted[None], axis=1) * ensemble_scale
    for step_index in range(STEPS):
        back = back + laplace(backward_rim(diffusivity * back))
    return control + back


def solution(mesh):
    placed = (
        P("mem", None, "gy", "gx"),
        P("mem", None, None, "gy", "gx"),
        P(None, "gy", "gx"),
        P(),
        P(None, "gy", "gx"),
    )
    return jax.shard_map(
        shards, mesh=mesh, in_specs=placed, out_specs=P("mem", None, "gy", "gx"), check_vma=False
    )
```

profile of v0, /device:TPU:486, one launch (start us, length us, event | category | flops | bytes accessed | tf_op | source)
XLA Modules:
  0.0 504.3 jit_solution(12866170469064015386)
XLA Ops:
  7.9 5.5 %collective-permute-start.1 = (f32[8,3,32,1]{3,2,1,0:T(8,128)S(1)}, f32[8,3,32,1]{3,2,1,0:T(8,128)S(1)}, u32[]{:S(2)}, u32[]{:S(2)}) collective-permute-start(f32[8,3,32,1]{3,2,1,0:T(8,128)S(1)} %get-tuple-element.41), channel_id=1, source_target_pairs={{16,0},{32,16},{48,32},{17,1},{33,17},{49,33},{18,2},{34,18},{50,3... | collective-permute-start | bytes 9224 | tf_op jit(solution)/shard_map/ppermute | solution.py:19
  14.7 7.2 %collective-permute-done.1 = f32[8,3,32,1]{3,2,1,0:T(8,128)S(1)} collective-permute-done((f32[8,3,32,1]{3,2,1,0:T(8,128)S(1)}, f32[8,3,32,1]{3,2,1,0:T(8,128)S(1)}, u32[]{:S(2)}, u32[]{:S(2)}) %collective-permute-start.1) | collective-permute-done | bytes 3104 | tf_op jit(solution)/shard_map/ppermute | solution.py:19
  21.8 31.4 %collective-permute-done = f32[8,3,32,1]{3,2,1,0:T(8,128)S(1)} collective-permute-done((f32[8,3,32,1]{3,2,1,0:T(8,128)S(1)}, f32[8,3,32,1]{3,2,1,0:T(8,128)S(1)}, u32[]{:S(2)}, u32[]{:S(2)}) %collective-permute-start) | collective-permute-done | bytes 3104 | tf_op jit(solution)/shard_map/ppermute | solution.py:18
  55.4 3.9 collective-permute-start.3
  68.6 6.2 %collective-permute-done.5 = f32[8,3,32,1]{3,2,1,0:T(8,128)S(1)} collective-permute-done((f32[8,3,32,1]{3,2,1,0:T(8,128)S(1)}, f32[8,3,32,1]{3,2,1,0:T(8,128)S(1)}, u32[]{:S(2)}, u32[]{:S(2)}) %collective-permute-start.5) | collective-permute-done | bytes 3104 | tf_op jit(solution)/shard_map/ppermute | solution.py:19
  74.8 27.3 %collective-permute-done.4 = f32[8,3,32,1]{3,2,1,0:T(8,128)S(1)} collective-permute-done((f32[8,3,32,1]{3,2,1,0:T(8,128)S(1)}, f32[8,3,32,1]{3,2,1,0:T(8,128)S(1)}, u32[]{:S(2)}, u32[]{:S(2)}) %collective-permute-start.4) | collective-permute-done | bytes 3104 | tf_op jit(solution)/shard_map/ppermute | solution.py:18
  104.2 3.9 collective-permute-start.7
  117.3 5.8 %collective-permute-done.9 = f32[8,3,32,1]{3,2,1,0:T(8,128)S(1)} collective-permute-done((f32[8,3,32,1]{3,2,1,0:T(8,128)S(1)}, f32[8,3,32,1]{3,2,1,0:T(8,128)S(1)}, u32[]{:S(2)}, u32[]{:S(2)}) %collective-permute-start.9) | collective-permute-done | bytes 3104 | tf_op jit(solution)/shard_map/ppermute | solution.py:19
  123.1 21.5 %collective-permute-done.8 = f32[8,3,32,1]{3,2,1,0:T(8,128)S(1)} collective-permute-done((f32[8,3,32,1]{3,2,1,0:T(8,128)S(1)}, f32[8,3,32,1]{3,2,1,0:T(8,128)S(1)}, u32[]{:S(2)}, u32[]{:S(2)}) %collective-permute-start.8) | collective-permute-done | bytes 3104 | tf_op jit(solution)/shard_map/ppermute | solution.py:18
  146.7 3.9 collective-permute-start.11
  155.4 4.0 collective-permute-start.13
  160.7 6.1 %collective-permute-done.13 = f32[8,3,32,1]{3,2,1,0:T(8,128)S(1)} collective-permute-done((f32[8,3,32,1]{3,2,1,0:T(8,128)S(1)}, f32[8,3,32,1]{3,2,1,0:T(8,128)S(1)}, u32[]{:S(2)}, u32[]{:S(2)}) %collective-permute-start.13) | collective-permute-done | bytes 3104 | tf_op jit(solution)/shard_map/ppermute | solution.py:19
  166.8 29.2 %collective-permute-done.12 = f32[8,3,32,1]{3,2,1,0:T(8,128)S(1)} collective-permute-done((f32[8,3,32,1]{3,2,1,0:T(8,128)S(1)}, f32[8,3,32,1]{3,2,1,0:T(8,128)S(1)}, u32[]{:S(2)}, u32[]{:S(2)}) %collective-permute-start.12) | collective-permute-done | bytes 3104 | tf_op jit(solution)/shard_map/ppermute | solution.py:18
  198.2 3.9 collective-permute-start.15
  207.8 71.1 %all-reduce.2.cloned.1.call-done = f32[6,3,32,128]{3,2,1,0:T(8,128)} async-done(((f32[6,3,32,128]{3,2,1,0:T(8,128)}), f32[6,3,32,128]{3,2,1,0:T(8,128)}) %all-reduce.2.cloned.1.call-update) | async-done | bytes 294928 | tf_op jit(solution)/shard_map/psum | solution.py:50
  280.4 6.9 %collective-permute-start.17 = (f32[8,3,32,1]{3,2,1,0:T(8,128)S(1)}, f32[8,3,32,1]{3,2,1,0:T(8,128)S(1)}, u32[]{:S(2)}, u32[]{:S(2)}) collective-permute-start(f32[8,3,32,1]{3,2,1,0:T(8,128)S(1)} %get-tuple-element.33), channel_id=1, source_target_pairs={{16,0},{32,16},{48,32},{17,1},{33,17},{49,33},{18,2},{34,18},{50,3... | collective-permute-start | bytes 9224 | tf_op jit(solution)/shard_map/ppermute | solution.py:19
  288.6 8.1 %collective-permute-done.17 = f32[8,3,32,1]{3,2,1,0:T(8,128)S(1)} collective-permute-done((f32[8,3,32,1]{3,2,1,0:T(8,128)S(1)}, f32[8,3,32,1]{3,2,1,0:T(8,128)S(1)}, u32[]{:S(2)}, u32[]{:S(2)}) %collective-permute-start.17) | collective-permute-done | bytes 3104 | tf_op jit(solution)/shard_map/ppermute | solution.py:19
  296.7 33.3 %collective-permute-done.16 = f32[8,3,32,1]{3,2,1,0:T(8,128)S(1)} collective-permute-done((f32[8,3,32,1]{3,2,1,0:T(8,128)S(1)}, f32[8,3,32,1]{3,2,1,0:T(8,128)S(1)}, u32[]{:S(2)}, u32[]{:S(2)}) %collective-permute-start.16) | collective-permute-done | bytes 3104 | tf_op jit(solution)/shard_map/ppermute | solution.py:18
  332.2 3.9 collective-permute-start.19
  340.8 7.9 %collective-permute-start.21 = (f32[8,3,32,1]{3,2,1,0:T(8,128)S(1)}, f32[8,3,32,1]{3,2,1,0:T(8,128)S(1)}, u32[]{:S(2)}, u32[]{:S(2)}) collective-permute-start(f32[8,3,32,1]{3,2,1,0:T(8,128)S(1)} %get-tuple-element.31), channel_id=1, source_target_pairs={{16,0},{32,16},{48,32},{17,1},{33,17},{49,33},{18,2},{34,18},{50,3... | collective-permute-start | bytes 9224 | tf_op jit(solution)/shard_map/ppermute | solution.py:19
  350.1 5.9 %collective-permute-done.21 = f32[8,3,32,1]{3,2,1,0:T(8,128)S(1)} collective-permute-done((f32[8,3,32,1]{3,2,1,0:T(8,128)S(1)}, f32[8,3,32,1]{3,2,1,0:T(8,128)S(1)}, u32[]{:S(2)}, u32[]{:S(2)}) %collective-permute-start.21) | collective-permute-done | bytes 3104 | tf_op jit(solution)/shard_map/ppermute | solution.py:19
  356.0 28.2 %collective-permute-done.20 = f32[8,3,32,1]{3,2,1,0:T(8,128)S(1)} collective-permute-done((f32[8,3,32,1]{3,2,1,0:T(8,128)S(1)}, f32[8,3,32,1]{3,2,1,0:T(8,128)S(1)}, u32[]{:S(2)}, u32[]{:S(2)}) %collective-permute-start.20) | collective-permute-done | bytes 3104 | tf_op jit(solution)/shard_map/ppermute | solution.py:18
  386.3 3.9 collective-permute-start.23
  395.0 9.3 %collective-permute-start.25 = (f32[8,3,32,1]{3,2,1,0:T(8,128)S(1)}, f32[8,3,32,1]{3,2,1,0:T(8,128)S(1)}, u32[]{:S(2)}, u32[]{:S(2)}) collective-permute-start(f32[8,3,32,1]{3,2,1,0:T(8,128)S(1)} %get-tuple-element.29), channel_id=1, source_target_pairs={{16,0},{32,16},{48,32},{17,1},{33,17},{49,33},{18,2},{34,18},{50,3... | collective-permute-start | bytes 9224 | tf_op jit(solution)/shard_map/ppermute | solution.py:19
  405.6 4.0 collective-permute-done.25
  409.6 22.2 %collective-permute-done.24 = f32[8,3,32,1]{3,2,1,0:T(8,128)S(1)} collective-permute-done((f32[8,3,32,1]{3,2,1,0:T(8,128)S(1)}, f32[8,3,32,1]{3,2,1,0:T(8,128)S(1)}, u32[]{:S(2)}, u32[]{:S(2)}) %collective-permute-start.24) | collective-permute-done | bytes 3104 | tf_op jit(solution)/shard_map/ppermute | solution.py:18
  432.0 4.5 collective-permute-start.26
  438.4 5.9 %collective-permute-done.27 = f32[8,3,1,130]{3,2,1,0:T(1,128)S(1)} collective-permute-done((f32[8,3,1,130]{3,2,1,0:T(1,128)S(1)}, f32[8,3,1,130]{3,2,1,0:T(1,128)S(1)}, u32[]{:S(2)}, u32[]{:S(2)}) %collective-permute-start.27) | collective-permute-done | bytes 12512 | tf_op jit(solution)/shard_map/ppermute | solution.py:18
  447.8 4.9 collective-permute-done.29
  452.6 28.1 %collective-permute-done.28 = f32[8,3,32,1]{3,2,1,0:T(8,128)S(1)} collective-permute-done((f32[8,3,32,1]{3,2,1,0:T(8,128)S(1)}, f32[8,3,32,1]{3,2,1,0:T(8,128)S(1)}, u32[]{:S(2)}, u32[]{:S(2)}) %collective-permute-start.28) | collective-permute-done | bytes 3104 | tf_op jit(solution)/shard_map/ppermute | solution.py:18
  480.9 7.3 %collective-permute-start.30 = (f32[8,3,1,130]{3,2,1,0:T(1,128)S(1)}, f32[8,3,1,130]{3,2,1,0:T(1,128)S(1)}, u32[]{:S(2)}, u32[]{:S(2)}) collective-permute-start(f32[8,3,1,130]{3,2,1,0:T(1,128)S(1)} %get-tuple-element.11), channel_id=1, source_target_pairs={{1,0},{2,1},{3,2},{4,3},{5,4},{6,5},{7,6},{8,7},{9,8},{10,9},{11,1... | collective-permute-start | bytes 37448 | tf_op jit(solution)/shard_map/ppermute | solution.py:19
  490.2 5.9 %collective-permute-done.31 = f32[8,3,1,130]{3,2,1,0:T(1,128)S(1)} collective-permute-done((f32[8,3,1,130]{3,2,1,0:T(1,128)S(1)}, f32[8,3,1,130]{3,2,1,0:T(1,128)S(1)}, u32[]{:S(2)}, u32[]{:S(2)}) %collective-permute-start.31) | collective-permute-done | bytes 12512 | tf_op jit(solution)/shard_map/ppermute | solution.py:18
  (76 shorter events, 69.3 us)
Async XLA Ops:
  6.5 272.3 %all-reduce.2.cloned.1.call-start = ((), (), s32[]{:S(2)}) async-start(), calls=%async_computation | async-start | bytes 589824 | tf_op jit(solution)/shard_map/psum | solution.py:50
  7.9 13.9 %collective-permute-start.1 = (f32[8,3,32,1]{3,2,1,0:T(8,128)S(1)}, f32[8,3,32,1]{3,2,1,0:T(8,128)S(1)}, u32[]{:S(2)}, u32[]{:S(2)}) collective-permute-start(f32[8,3,32,1]{3,2,1,0:T(8,128)S(1)} %get-tuple-element.41), channel_id=1, source_target_pairs={{16,0},{32,16},{48,32},{17,1},{33,17},{49,33},{18,2},{34,18},{50,3... | collective-permute-start | bytes 9224 | tf_op jit(solution)/shard_map/ppermute | solution.py:19
  13.4 39.9 %collective-permute-start = (f32[8,3,32,1]{3,2,1,0:T(8,128)S(1)}, f32[8,3,32,1]{3,2,1,0:T(8,128)S(1)}, u32[]{:S(2)}, u32[]{:S(2)}) collective-permute-start(f32[8,3,32,1]{3,2,1,0:T(8,128)S(1)} %get-tuple-element.42), channel_id=1, source_target_pairs={{0,16},{16,32},{32,48},{1,17},{17,33},{33,49},{2,18},{18,34},{34,5... | collective-permute-start | bytes 9224 | tf_op jit(solution)/shard_map/ppermute | solution.py:18
  53.5 5.9 %collective-permute-start.2 = (f32[8,3,1,130]{3,2,1,0:T(1,128)S(1)}, f32[8,3,1,130]{3,2,1,0:T(1,128)S(1)}, u32[]{:S(2)}, u32[]{:S(2)}) collective-permute-start(f32[8,3,1,130]{3,2,1,0:T(1,128)S(1)} %get-tuple-element.25), channel_id=1, source_target_pairs={{1,0},{2,1},{3,2},{4,3},{5,4},{6,5},{7,6},{8,7},{9,8},{10,9},{11,1... | collective-permute-start | bytes 37448 | tf_op jit(solution)/shard_map/ppermute | solution.py:19
  55.4 7.8 %collective-permute-start.3 = (f32[8,3,1,130]{3,2,1,0:T(1,128)S(1)}, f32[8,3,1,130]{3,2,1,0:T(1,128)S(1)}, u32[]{:S(2)}, u32[]{:S(2)}) collective-permute-start(f32[8,3,1,130]{3,2,1,0:T(1,128)S(1)} %get-tuple-element.26), channel_id=1, source_target_pairs={{0,1},{1,2},{2,3},{3,4},{4,5},{5,6},{6,7},{7,8},{8,9},{9,10},{10,1... | collective-permute-start | bytes 37448 | tf_op jit(solution)/shard_map/ppermute | solution.py:18
  64.1 10.7 %collective-permute-start.5 = (f32[8,3,32,1]{3,2,1,0:T(8,128)S(1)}, f32[8,3,32,1]{3,2,1,0:T(8,128)S(1)}, u32[]{:S(2)}, u32[]{:S(2)}) collective-permute-start(f32[8,3,32,1]{3,2,1,0:T(8,128)S(1)} %get-tuple-element.39), channel_id=1, source_target_pairs={{16,0},{32,16},{48,32},{17,1},{33,17},{49,33},{18,2},{34,18},{50,3... | collective-permute-start | bytes 9224 | tf_op jit(solution)/shard_map/ppermute | solution.py:19
  67.3 34.8 %collective-permute-start.4 = (f32[8,3,32,1]{3,2,1,0:T(8,128)S(1)}, f32[8,3,32,1]{3,2,1,0:T(8,128)S(1)}, u32[]{:S(2)}, u32[]{:S(2)}) collective-permute-start(f32[8,3,32,1]{3,2,1,0:T(8,128)S(1)} %get-tuple-element.40), channel_id=1, source_target_pairs={{0,16},{16,32},{32,48},{1,17},{17,33},{33,49},{2,18},{18,34},{34,5... | collective-permute-start | bytes 9224 | tf_op jit(solution)/shard_map/ppermute | solution.py:18
  102.3 5.9 %collective-permute-start.6 = (f32[8,3,1,130]{3,2,1,0:T(1,128)S(1)}, f32[8,3,1,130]{3,2,1,0:T(1,128)S(1)}, u32[]{:S(2)}, u32[]{:S(2)}) collective-permute-start(f32[8,3,1,130]{3,2,1,0:T(1,128)S(1)} %get-tuple-element.23), channel_id=1, source_target_pairs={{1,0},{2,1},{3,2},{4,3},{5,4},{6,5},{7,6},{8,7},{9,8},{10,9},{11,1... | collective-permute-start | bytes 37448 | tf_op jit(solution)/shard_map/ppermute | solution.py:19
  104.2 7.8 %collective-permute-start.7 = (f32[8,3,1,130]{3,2,1,0:T(1,128)S(1)}, f32[8,3,1,130]{3,2,1,0:T(1,128)S(1)}, u32[]{:S(2)}, u32[]{:S(2)}) collective-permute-start(f32[8,3,1,130]{3,2,1,0:T(1,128)S(1)} %get-tuple-element.24), channel_id=1, source_target_pairs={{0,1},{1,2},{2,3},{3,4},{4,5},{5,6},{6,7},{7,8},{8,9},{9,10},{10,1... | collective-permute-start | bytes 37448 | tf_op jit(solution)/shard_map/ppermute | solution.py:18
  112.9 10.2 %collective-permute-start.9 = (f32[8,3,32,1]{3,2,1,0:T(8,128)S(1)}, f32[8,3,32,1]{3,2,1,0:T(8,128)S(1)}, u32[]{:S(2)}, u32[]{:S(2)}) collective-permute-start(f32[8,3,32,1]{3,2,1,0:T(8,128)S(1)} %get-tuple-element.37), channel_id=1, source_target_pairs={{16,0},{32,16},{48,32},{17,1},{33,17},{49,33},{18,2},{34,18},{50,3... | collective-permute-start | bytes 9224 | tf_op jit(solution)/shard_map/ppermute | solution.py:19
  116.0 28.6 %collective-permute-start.8 = (f32[8,3,32,1]{3,2,1,0:T(8,128)S(1)}, f32[8,3,32,1]{3,2,1,0:T(8,128)S(1)}, u32[]{:S(2)}, u32[]{:S(2)}) collective-permute-start(f32[8,3,32,1]{3,2,1,0:T(8,128)S(1)} %get-tuple-element.38), channel_id=1, source_target_pairs={{0,16},{16,32},{32,48},{1,17},{17,33},{33,49},{2,18},{18,34},{34,5... | collective-permute-start | bytes 9224 | tf_op jit(solution)/shard_map/ppermute | solution.py:18
  144.8 5.9 %collective-permute-start.10 = (f32[8,3,1,130]{3,2,1,0:T(1,128)S(1)}, f32[8,3,1,130]{3,2,1,0:T(1,128)S(1)}, u32[]{:S(2)}, u32[]{:S(2)}) collective-permute-start(f32[8,3,1,130]{3,2,1,0:T(1,128)S(1)} %get-tuple-element.21), channel_id=1, source_target_pairs={{1,0},{2,1},{3,2},{4,3},{5,4},{6,5},{7,6},{8,7},{9,8},{10,9},{11,1... | collective-permute-start | bytes 37448 | tf_op jit(solution)/shard_map/ppermute | solution.py:19
  146.7 7.8 %collective-permute-start.11 = (f32[8,3,1,130]{3,2,1,0:T(1,128)S(1)}, f32[8,3,1,130]{3,2,1,0:T(1,128)S(1)}, u32[]{:S(2)}, u32[]{:S(2)}) collective-permute-start(f32[8,3,1,130]{3,2,1,0:T(1,128)S(1)} %get-tuple-element.22), channel_id=1, source_target_pairs={{0,1},{1,2},{2,3},{3,4},{4,5},{5,6},{6,7},{7,8},{8,9},{9,10},{10,1... | collective-permute-start | bytes 37448 | tf_op jit(solution)/shard_map/ppermute | solution.py:18
  155.4 11.4 %collective-permute-start.13 = (f32[8,3,32,1]{3,2,1,0:T(8,128)S(1)}, f32[8,3,32,1]{3,2,1,0:T(8,128)S(1)}, u32[]{:S(2)}, u32[]{:S(2)}) collective-permute-start(f32[8,3,32,1]{3,2,1,0:T(8,128)S(1)} %get-tuple-element.35), channel_id=1, source_target_pairs={{16,0},{32,16},{48,32},{17,1},{33,17},{49,33},{18,2},{34,18},{50,3... | collective-permute-start | bytes 9224 | tf_op jit(solution)/shard_map/ppermute | solution.py:19
  159.4 36.6 %collective-permute-start.12 = (f32[8,3,32,1]{3,2,1,0:T(8,128)S(1)}, f32[8,3,32,1]{3,2,1,0:T(8,128)S(1)}, u32[]{:S(2)}, u32[]{:S(2)}) collective-permute-start(f32[8,3,32,1]{3,2,1,0:T(8,128)S(1)} %get-tuple-element.36), channel_id=1, source_target_pairs={{0,16},{16,32},{32,48},{1,17},{17,33},{33,49},{2,18},{18,34},{34,5... | collective-permute-start | bytes 9224 | tf_op jit(solution)/shard_map/ppermute | solution.py:18
  196.2 6.0 %collective-permute-start.14 = (f32[8,3,1,130]{3,2,1,0:T(1,128)S(1)}, f32[8,3,1,130]{3,2,1,0:T(1,128)S(1)}, u32[]{:S(2)}, u32[]{:S(2)}) collective-permute-start(f32[8,3,1,130]{3,2,1,0:T(1,128)S(1)} %get-tuple-element.19), channel_id=1, source_target_pairs={{1,0},{2,1},{3,2},{4,3},{5,4},{6,5},{7,6},{8,7},{9,8},{10,9},{11,1... | collective-permute-start | bytes 37448 | tf_op jit(solution)/shard_map/ppermute | solution.py:19
  198.2 7.8 %collective-permute-start.15 = (f32[8,3,1,130]{3,2,1,0:T(1,128)S(1)}, f32[8,3,1,130]{3,2,1,0:T(1,128)S(1)}, u32[]{:S(2)}, u32[]{:S(2)}) collective-permute-start(f32[8,3,1,130]{3,2,1,0:T(1,128)S(1)} %get-tuple-element.20), channel_id=1, source_target_pairs={{0,1},{1,2},{2,3},{3,4},{4,5},{5,6},{6,7},{7,8},{8,9},{9,10},{10,1... | collective-permute-start | bytes 37448 | tf_op jit(solution)/shard_map/ppermute | solution.py:18
  280.4 16.3 %collective-permute-start.17 = (f32[8,3,32,1]{3,2,1,0:T(8,128)S(1)}, f32[8,3,32,1]{3,2,1,0:T(8,128)S(1)}, u32[]{:S(2)}, u32[]{:S(2)}) collective-permute-start(f32[8,3,32,1]{3,2,1,0:T(8,128)S(1)} %get-tuple-element.33), channel_id=1, source_target_pairs={{16,0},{32,16},{48,32},{17,1},{33,17},{49,33},{18,2},{34,18},{50,3... | collective-permute-start | bytes 9224 | tf_op jit(solution)/shard_map/ppermute | solution.py:19
  287.3 42.7 %collective-permute-start.16 = (f32[8,3,32,1]{3,2,1,0:T(8,128)S(1)}, f32[8,3,32,1]{3,2,1,0:T(8,128)S(1)}, u32[]{:S(2)}, u32[]{:S(2)}) collective-permute-start(f32[8,3,32,1]{3,2,1,0:T(8,128)S(1)} %get-tuple-element.34), channel_id=1, source_target_pairs={{0,16},{16,32},{32,48},{1,17},{17,33},{33,49},{2,18},{18,34},{34,5... | collective-permute-start | bytes 9224 | tf_op jit(solution)/shard_map/ppermute | solution.py:18
  330.3 5.9 %collective-permute-start.18 = (f32[8,3,1,130]{3,2,1,0:T(1,128)S(1)}, f32[8,3,1,130]{3,2,1,0:T(1,128)S(1)}, u32[]{:S(2)}, u32[]{:S(2)}) collective-permute-start(f32[8,3,1,130]{3,2,1,0:T(1,128)S(1)} %get-tuple-element.17), channel_id=1, source_target_pairs={{1,0},{2,1},{3,2},{4,3},{5,4},{6,5},{7,6},{8,7},{9,8},{10,9},{11,1... | collective-permute-start | bytes 37448 | tf_op jit(solution)/shard_map/ppermute | solution.py:19
  332.2 7.8 %collective-permute-start.19 = (f32[8,3,1,130]{3,2,1,0:T(1,128)S(1)}, f32[8,3,1,130]{3,2,1,0:T(1,128)S(1)}, u32[]{:S(2)}, u32[]{:S(2)}) collective-permute-start(f32[8,3,1,130]{3,2,1,0:T(1,128)S(1)} %get-tuple-element.18), channel_id=1, source_target_pairs={{0,1},{1,2},{2,3},{3,4},{4,5},{5,6},{6,7},{7,8},{8,9},{9,10},{10,1... | collective-permute-start | bytes 37448 | tf_op jit(solution)/shard_map/ppermute | solution.py:18
  340.8 15.1 %collective-permute-start.21 = (f32[8,3,32,1]{3,2,1,0:T(8,128)S(1)}, f32[8,3,32,1]{3,2,1,0:T(8,128)S(1)}, u32[]{:S(2)}, u32[]{:S(2)}) collective-permute-start(f32[8,3,32,1]{3,2,1,0:T(8,128)S(1)} %get-tuple-element.31), channel_id=1, source_target_pairs={{16,0},{32,16},{48,32},{17,1},{33,17},{49,33},{18,2},{34,18},{50,3... | collective-permute-start | bytes 9224 | tf_op jit(solution)/shard_map/ppermute | solution.py:19
  348.8 35.4 %collective-permute-start.20 = (f32[8,3,32,1]{3,2,1,0:T(8,128)S(1)}, f32[8,3,32,1]{3,2,1,0:T(8,128)S(1)}, u32[]{:S(2)}, u32[]{:S(2)}) collective-permute-start(f32[8,3,32,1]{3,2,1,0:T(8,128)S(1)} %get-tuple-element.32), channel_id=1, source_target_pairs={{0,16},{16,32},{32,48},{1,17},{17,33},{33,49},{2,18},{18,34},{34,5... | collective-permute-start | bytes 9224 | tf_op jit(solution)/shard_map/ppermute | solution.py:18
  386.3 7.8 %collective-permute-start.23 = (f32[8,3,1,130]{3,2,1,0:T(1,128)S(1)}, f32[8,3,1,130]{3,2,1,0:T(1,128)S(1)}, u32[]{:S(2)}, u32[]{:S(2)}) collective-permute-start(f32[8,3,1,130]{3,2,1,0:T(1,128)S(1)} %get-tuple-element.16), channel_id=1, source_target_pairs={{0,1},{1,2},{2,3},{3,4},{4,5},{5,6},{6,7},{7,8},{8,9},{9,10},{10,1... | collective-permute-start | bytes 37448 | tf_op jit(solution)/shard_map/ppermute | solution.py:18
  395.0 14.7 %collective-permute-start.25 = (f32[8,3,32,1]{3,2,1,0:T(8,128)S(1)}, f32[8,3,32,1]{3,2,1,0:T(8,128)S(1)}, u32[]{:S(2)}, u32[]{:S(2)}) collective-permute-start(f32[8,3,32,1]{3,2,1,0:T(8,128)S(1)} %get-tuple-element.29), channel_id=1, source_target_pairs={{16,0},{32,16},{48,32},{17,1},{33,17},{49,33},{18,2},{34,18},{50,3... | collective-permute-start | bytes 9224 | tf_op jit(solution)/shard_map/ppermute | solution.py:19
  404.3 27.5 %collective-permute-start.24 = (f32[8,3,32,1]{3,2,1,0:T(8,128)S(1)}, f32[8,3,32,1]{3,2,1,0:T(8,128)S(1)}, u32[]{:S(2)}, u32[]{:S(2)}) collective-permute-start(f32[8,3,32,1]{3,2,1,0:T(8,128)S(1)} %get-tuple-element.30), channel_id=1, source_target_pairs={{0,16},{16,32},{32,48},{1,17},{17,33},{33,49},{2,18},{18,34},{34,5... | collective-permute-start | bytes 9224 | tf_op jit(solution)/shard_map/ppermute | solution.py:18
  432.0 6.4 %collective-permute-start.26 = (f32[8,3,1,130]{3,2,1,0:T(1,128)S(1)}, f32[8,3,1,130]{3,2,1,0:T(1,128)S(1)}, u32[]{:S(2)}, u32[]{:S(2)}) collective-permute-start(f32[8,3,1,130]{3,2,1,0:T(1,128)S(1)} %get-tuple-element.13), channel_id=1, source_target_pairs={{1,0},{2,1},{3,2},{4,3},{5,4},{6,5},{7,6},{8,7},{9,8},{10,9},{11,1... | collective-permute-start | bytes 37448 | tf_op jit(solution)/shard_map/ppermute | solution.py:19
  436.5 7.8 %collective-permute-start.27 = (f32[8,3,1,130]{3,2,1,0:T(1,128)S(1)}, f32[8,3,1,130]{3,2,1,0:T(1,128)S(1)}, u32[]{:S(2)}, u32[]{:S(2)}) collective-permute-start(f32[8,3,1,130]{3,2,1,0:T(1,128)S(1)} %get-tuple-element.14), channel_id=1, source_target_pairs={{0,1},{1,2},{2,3},{3,4},{4,5},{5,6},{6,7},{7,8},{8,9},{9,10},{10,1... | collective-permute-start | bytes 37448 | tf_op jit(solution)/shard_map/ppermute | solution.py:18
  445.1 7.5 %collective-permute-start.29 = (f32[8,3,32,1]{3,2,1,0:T(8,128)S(1)}, f32[8,3,32,1]{3,2,1,0:T(8,128)S(1)}, u32[]{:S(2)}, u32[]{:S(2)}) collective-permute-start(f32[8,3,32,1]{3,2,1,0:T(8,128)S(1)} %get-tuple-element.27), channel_id=1, source_target_pairs={{16,0},{32,16},{48,32},{17,1},{33,17},{49,33},{18,2},{34,18},{50,3... | collective-permute-start | bytes 9224 | tf_op jit(solution)/shard_map/ppermute | solution.py:19
  446.5 34.2 %collective-permute-start.28 = (f32[8,3,32,1]{3,2,1,0:T(8,128)S(1)}, f32[8,3,32,1]{3,2,1,0:T(8,128)S(1)}, u32[]{:S(2)}, u32[]{:S(2)}) collective-permute-start(f32[8,3,32,1]{3,2,1,0:T(8,128)S(1)} %get-tuple-element.28), channel_id=1, source_target_pairs={{0,16},{16,32},{32,48},{1,17},{17,33},{33,49},{2,18},{18,34},{34,5... | collective-permute-start | bytes 9224 | tf_op jit(solution)/shard_map/ppermute | solution.py:18
  480.9 9.2 %collective-permute-start.30 = (f32[8,3,1,130]{3,2,1,0:T(1,128)S(1)}, f32[8,3,1,130]{3,2,1,0:T(1,128)S(1)}, u32[]{:S(2)}, u32[]{:S(2)}) collective-permute-start(f32[8,3,1,130]{3,2,1,0:T(1,128)S(1)} %get-tuple-element.11), channel_id=1, source_target_pairs={{1,0},{2,1},{3,2},{4,3},{5,4},{6,5},{7,6},{8,7},{9,8},{10,9},{11,1... | collective-permute-start | bytes 37448 | tf_op jit(solution)/shard_map/ppermute | solution.py:19
  488.2 7.8 %collective-permute-start.31 = (f32[8,3,1,130]{3,2,1,0:T(1,128)S(1)}, f32[8,3,1,130]{3,2,1,0:T(1,128)S(1)}, u32[]{:S(2)}, u32[]{:S(2)}) collective-permute-start(f32[8,3,1,130]{3,2,1,0:T(1,128)S(1)} %get-tuple-element.12), channel_id=1, source_target_pairs={{0,1},{1,2},{2,3},{3,4},{4,5},{5,6},{6,7},{7,8},{8,9},{9,10},{10,1... | collective-permute-start | bytes 37448 | tf_op jit(solution)/shard_map/ppermute | solution.py:18
  (6 other events, 238.9 us)
Sparse Core Ops, SparseCore 0:
  207.9 70.9 all-reduce.1
where the time goes:
time: 505 us; the launch traced here: 504 us
  waiting for transfers between devices  375 us (74%)
  starting transfers between devices  102 us (20%)
  between operations  13.9 us (3%)
  other arithmetic  9.9 us (2%)
    ppermute x16, waiting for transfers between devices, padded_2(): before = lax.ppermute(last, axis, up)  256 us
    psum x1, waiting for transfers between devices, shards(): increment = lax.psum(member_terms, 'mem')  71.1 us
    ppermute x16, starting transfers between devices, padded_2(): after = lax.ppermute(initial, axis, down)  64.7 us
    ppermute x16, waiting for transfers between devices, padded_2(): after = lax.ppermute(initial, axis, down)  48.2 us
    ppermute x16, starting transfers between devices, padded_2(): before = lax.ppermute(last, axis, up)  37.7 us
  transfers between devices with their start and end apart: 33, of which 25 were waited for; matrix products, arithmetic and copies ran while one was open for 0% of the time, Pallas kernels for 0%

commit v1 on v0

v1 whole, which is shorter than its diff:
```python
import math

import jax
import jax.numpy as jnp
from jax import lax
from jax.experimental import pallas as pl
from jax.experimental.pallas import tpu as pltpu
from jax.sharding import PartitionSpec as P

STEPS = 4
LANES = 128


def exchange(last, first, axis):
    size = lax.axis_size(axis)
    up = [(i, i + 1) for i in range(size - 1)]
    down = [(j, i) for i, j in up]
    return lax.ppermute(last, axis, up), lax.ppermute(first, axis, down)


def lane_ids(rows):
    return lax.broadcasted_iota(jnp.int32, (rows, LANES), 1)


def pack_columns(planes, rows):
    group = lane_ids(rows) // STEPS
    first = jnp.zeros((rows, LANES), jnp.float32)
    last = jnp.zeros((rows, LANES), jnp.float32)
    for p, plane in enumerate(planes):
        first = jnp.where(group == p, pltpu.roll(plane, (STEPS * p) % LANES, 1), first)
        last = jnp.where(group == p, pltpu.roll(plane, (STEPS * p + STEPS) % LANES, 1), last)
    return first, last


def pack_kernel(control, diffusivity, first, last):
    count, rows, _ = control.shape
    planes = [control[p] for p in range(count)] + [diffusivity[l] for l in range(diffusivity.shape[0])]
    first[...], last[...] = pack_columns(planes, rows)


def side_lanes(west, east, p, rows):
    lane = lane_ids(rows)
    east_part = pltpu.roll(east, lax.rem(2 * LANES - STEPS * p, LANES), 1)
    west_part = pltpu.roll(west, lax.rem(2 * LANES - STEPS - STEPS * p, LANES), 1)
    return jnp.where(lane < STEPS, east_part, jnp.where(lane >= LANES - STEPS, west_part, 0.0))


def widened(main, sides, rim, rim_sides):
    top = jnp.concatenate([main, rim], axis=0)
    side = jnp.concatenate([sides, rim_sides], axis=0)
    return jnp.concatenate([top, side], axis=1)


def neighbours(field):
    rows, lanes = field.shape
    return (
        pltpu.roll(field, 1, 0)
        + pltpu.roll(field, rows - 1, 0)
        + pltpu.roll(field, 1, 1)
        + pltpu.roll(field, lanes - 1, 1)
    )


def spread_kernel(levels, control, diffusivity, west, east, rim, perturb, partial, wide_diff, spread):
    count, rows, _ = control.shape
    members = count // levels
    variables = perturb.shape[1]

    def wide(main, p):
        sides = side_lanes(west[...], east[...], p, rows)
        rim_sides = side_lanes(rim[count + levels], rim[count + levels + 1], p, 2 * STEPS)
        return widened(main, sides, rim[p], rim_sides)

    for l in range(levels):
        wide_diff[l] = wide(diffusivity[l], count + l)

    def one(m, carry):
        for l in range(levels):
            field = wide(control[m * levels + l], m * levels + l)
            for _ in range(STEPS):
                field = field + wide_diff[l] * (neighbours(field) - 4.0 * field)
            spread[m * levels + l] = field[:rows, :LANES]
        return carry

    lax.fori_loop(0, members, one, 0)
    for v in range(variables):
        for l in range(levels):
            total = perturb[0, v, l].astype(jnp.float32) * spread[l]
            for m in range(1, members):
                total = total + perturb[m, v, l].astype(jnp.float32) * spread[m * levels + l]
            partial[v * levels + l] = total


def back_kernel(scale, increment, obs_count, obs_weight, perturb, back, first, last, weighted):
    members, variables, levels, rows, _ = perturb.shape
    for l in range(levels):
        seen = obs_count[l].astype(jnp.float32) * (scale * scale)
        for v in range(variables):
            weighted[v * levels + l] = seen * obs_weight[v] * increment[v * levels + l]
    planes = []
    for m in range(members):
        for l in range(levels):
            total = perturb[m, 0, l].astype(jnp.float32) * weighted[l]
            for v in range(1, variables):
                total = total + perturb[m, v, l].astype(jnp.float32) * weighted[v * levels + l]
            back[m * levels + l] = total
    planes = [back[p] for p in range(members * levels)]
    first[...], last[...] = pack_columns(planes, rows)


def adjoint_kernel(levels, control, back, wide_diff, west, east, rim, out):
    count, rows, _ = back.shape

    def one(m, carry):
        for l in range(levels):
            p = m * levels + l
            sides = side_lanes(west[...], east[...], p, rows)
            rim_sides = side_lanes(rim[count], rim[count + 1], p, 2 * STEPS)
            field = widened(back[p], sides, rim[p], rim_sides)
            for _ in range(STEPS):
                carried = wide_diff[l] * field
                field = field + (neighbours(carried) - 4.0 * carried)
            out[p] = control[p] + field[:rows, :LANES]
        return carry

    lax.fori_loop(0, count // levels, one, 0)


def shape_of(*shape):
    return jax.ShapeDtypeStruct(shape, jnp.float32)


def rim_rows(planes, west, east):
    south = jnp.concatenate([p[:, :STEPS] for p in planes] + [west[None, :STEPS], east[None, :STEPS]], axis=0)
    north = jnp.concatenate([p[:, -STEPS:] for p in planes] + [west[None, -STEPS:], east[None, -STEPS:]], axis=0)
    from_north, from_south = exchange(north, south, "gy")
    return jnp.concatenate([from_south, from_north], axis=1)


def shards(control, perturb, obs_count, obs_weight, diffusivity):
    members, levels, rows, columns = control.shape
    variables = perturb.shape[1]
    ways = lax.axis_size("mem")
    scale = 1.0 / math.sqrt(members * ways - 1)
    count = members * levels
    flat = control.reshape(count, rows, columns)

    first, last = pl.pallas_call(
        pack_kernel, out_shape=(shape_of(rows, LANES), shape_of(rows, LANES)), name="pack"
    )(flat, diffusivity)
    west, east = exchange(last, first, "gx")
    rim = rim_rows([flat, diffusivity], west, east)

    partial, wide_diff = pl.pallas_call(
        lambda *refs: spread_kernel(levels, *refs),
        out_shape=(shape_of(variables * levels, rows, columns), shape_of(levels, rows + 2 * STEPS, 2 * LANES)),
        scratch_shapes=[pltpu.VMEM((count, rows, columns), jnp.float32)],
        name="spread",
    )(flat, diffusivity, west, east, rim, perturb)

    parts = lax.all_to_all(partial.reshape(ways, -1, columns), "mem", 0, 0)
    mine = jnp.sum(parts, axis=0)
    increment = lax.all_to_all(jnp.broadcast_to(mine, parts.shape), "mem", 0, 0)
    increment = increment.reshape(variables * levels, rows, columns)

    back, first, last = pl.pallas_call(
        lambda *refs: back_kernel(scale, *refs),
        out_shape=(shape_of(count, rows, columns), shape_of(rows, LANES), shape_of(rows, LANES)),
        in_specs=[
            pl.BlockSpec(memory_space=pltpu.VMEM),
            pl.BlockSpec(memory_space=pltpu.VMEM),
            pl.BlockSpec(memory_space=pltpu.SMEM),
            pl.BlockSpec(memory_space=pltpu.VMEM),
        ],
        scratch_shapes=[pltpu.VMEM((variables * levels, rows, columns), jnp.float32)],
        name="back",
    )(increment, obs_count, obs_weight, perturb)
    west, east = exchange(last, first, "gx")
    rim = rim_rows([back], west, east)

    out = pl.pallas_call(
        lambda *refs: adjoint_kernel(levels, *refs),
        out_shape=shape_of(count, rows, columns),
        name="adjoint",
    )(flat, back, wide_diff, west, east, rim)
    return out.reshape(control.shape)


def solution(mesh):
    placed = (
        P("mem", None, "gy", "gx"),
        P("mem", None, None, "gy", "gx"),
        P(None, "gy", "gx"),
        P(),
        P(None, "gy", "gx"),
    )
    return jax.shard_map(
        shards, mesh=mesh, in_specs=placed, out_specs=P("mem", None, "gy", "gx"), check_vma=False
    )
```

time: 505 us -> 100 us (0.20)
  the two profiles are of different devices: /device:TPU:486 before, /device:TPU:24 now
where the time goes in v1:
time: 100 us; the launch traced here: 99.7 us
  starting transfers between devices  31.3 us (31%)
  waiting for transfers between devices  24.6 us (25%)
  blocking collectives  23.1 us (23%)
  Pallas kernels  16.5 us (16%)
  local copies, waits for them, and re-layouts  2.71 us (3%)
  other arithmetic  1.42 us (1%)
    ppermute x8, starting transfers between devices, exchange(): return (lax.ppermute(last, axis, up), lax.ppermute(first, axis, down))  31.3 us
    ppermute x8, waiting for transfers between devices, exchange(): return (lax.ppermute(last, axis, up), lax.ppermute(first, axis, down))  24.6 us
    all_to_all x1, blocking collectives, shards(): parts = lax.all_to_all(partial.reshape(ways, -1, columns), 'mem', 0, 0)  12.2 us
    all_to_all x1, blocking collectives, shards(): increment = lax.all_to_all(jnp.broadcast_to(mine, parts.shape), 'mem', 0, 0)  10.9 us
    pallas_call x1, Pallas kernels, shards(): pl.pallas_call(lambda *refs: spread_kernel(levels, *refs), out_shape=(sha...  6.35 us
    pallas_call x1, Pallas kernels, shards(): pl.pallas_call(lambda *refs: adjoint_kernel(levels, *refs), out_shape=sha...  5.82 us
    slice x3, local copies, waits for them, and re-layouts, rim_rows(): p[:, :STEPS]  2.65 us
    pallas_call x1, Pallas kernels, shards(): pl.pallas_call(lambda *refs: back_kernel(scale, *refs), out_shape=(shape_...  2.41 us
  transfers between devices with their start and end apart: 8, of which 6 were waited for; matrix products, arithmetic and copies ran while one was open for 3% of the time, Pallas kernels for 0%

profile of v1, /device:TPU:24, one launch (start us, length us, event | category | flops | bytes accessed | tf_op | source)
XLA Modules:
  0.0 99.7 jit_solution(17763168707282541524)
XLA Ops:
  0.0 1.9 %pack.1 = (f32[32,128]{1,0:T(8,128)}, f32[32,128]{1,0:T(8,128)}) custom-call(f32[24,32,128]{2,1,0:T(8,128)} %bitcast.20, f32[3,32,128]{2,1,0:T(8,128)} %refs_1_.2), custom_call_target="tpu_custom_call" | custom-call | tf_op jit(solution)/shard_map/pack/pallas_call | solution.py:148
  1.9 9.1 %collective-permute-start = (f32[32,128]{1,0:T(8,128)}, f32[32,128]{1,0:T(8,128)S(1)}, u32[]{:S(2)}, u32[]{:S(2)}) collective-permute-start(f32[32,128]{1,0:T(8,128)} %get-tuple-element.12), channel_id=1, source_target_pairs={{0,16},{16,32},{32,48},{1,17},{17,33},{33,49},{2,18},{18,34},{34,5... | collective-permute-start | bytes 49160 | tf_op jit(solution)/shard_map/ppermute | solution.py:18
  11.0 1.3 %collective-permute-start.1 = (f32[32,128]{1,0:T(8,128)}, f32[32,128]{1,0:T(8,128)S(1)}, u32[]{:S(2)}, u32[]{:S(2)}) collective-permute-start(f32[32,128]{1,0:T(8,128)} %get-tuple-element.13), channel_id=1, source_target_pairs={{16,0},{32,16},{48,32},{17,1},{33,17},{49,33},{18,2},{34,18},{50,3... | collective-permute-start | bytes 49160 | tf_op jit(solution)/shard_map/ppermute | solution.py:18
  12.3 1.0 fusion.1
  13.2 0.7 fusion.2
  14.0 0.0 collective-permute-done.refs_2_
  14.0 8.2 %collective-permute-done.1.refs_3_ = f32[32,128]{1,0:T(8,128)S(1)} collective-permute-done((f32[32,128]{1,0:T(8,128)}, f32[32,128]{1,0:T(8,128)S(1)}, u32[]{:S(2)}, u32[]{:S(2)}) %collective-permute-start.1) | collective-permute-done | bytes 16416 | tf_op jit(solution)/shard_map/ppermute | solution.py:18
  22.2 2.4 %collective-permute-start.3 = (f32[29,4,128]{2,1,0:T(4,128)S(1)}, f32[29,4,128]{2,1,0:T(4,128)S(1)}, u32[]{:S(2)}, u32[]{:S(2)}) collective-permute-start(f32[29,4,128]{2,1,0:T(4,128)S(1)} %pad_maximum_fusion.3), channel_id=1, source_target_pairs={{0,1},{1,2},{2,3},{3,4},{4,5},{5,6},{6,7},{7,8},{8,9},{9,10},{10,1... | collective-permute-start | bytes 178184 | tf_op jit(solution)/shard_map/ppermute | solution.py:18
  24.6 3.4 %collective-permute-start.2 = (f32[29,4,128]{2,1,0:T(4,128)S(1)}, f32[29,4,128]{2,1,0:T(4,128)S(1)}, u32[]{:S(2)}, u32[]{:S(2)}) collective-permute-start(f32[29,4,128]{2,1,0:T(4,128)S(1)} %pad_maximum_fusion.2), channel_id=1, source_target_pairs={{1,0},{2,1},{3,2},{4,3},{5,4},{6,5},{7,6},{8,7},{9,8},{10,9},{11,1... | collective-permute-start | bytes 178184 | tf_op jit(solution)/shard_map/ppermute | solution.py:18
  28.1 0.2 collective-permute-done.3
  28.3 4.6 %collective-permute-done.2 = f32[29,4,128]{2,1,0:T(4,128)S(1)} collective-permute-done((f32[29,4,128]{2,1,0:T(4,128)S(1)}, f32[29,4,128]{2,1,0:T(4,128)S(1)}, u32[]{:S(2)}, u32[]{:S(2)}) %collective-permute-start.2) | collective-permute-done | bytes 59424 | tf_op jit(solution)/shard_map/ppermute | solution.py:18
  32.8 0.7 pad_maximum_fusion.refs_4_
  33.5 0.0 copy-done
  33.5 0.0 copy-done.1
  33.5 6.3 %spread.1 = (f32[18,32,128]{2,1,0:T(8,128)}, f32[3,40,256]{2,1,0:T(8,128)}) custom-call(f32[24,32,128]{2,1,0:T(8,128)} %bitcast.22, f32[3,32,128]{2,1,0:T(8,128)} %refs_1_.2, f32[32,128]{1,0:T(8,128)} %copy-done, f32[32,128]{1,0:T(8,128)} %copy-done.1, f32[29,8,128]{2,1,0:T(8,128)} %pad_maximum_fusion.refs_4_, bf16[8,6,3,32,128]{4,3,2,1,0:T(8,128)(2,1)} %refs_3_.1), custom_call_target="tpu_custom_call" | custom-call | tf_op jit(solution)/shard_map/spread/pallas_call | solution.py:154
  39.9 12.2 %all_to_all.10 = f32[8,72,128]{2,1,0:T(8,128)S(1)} all-to-all(f32[8,72,128]{2,1,0:T(8,128)} %bitcast.25), channel_id=1, replica_groups=mesh['mem'=8,'gx'=4,'gy'=16] {'mem'}, dimensions={0} | all-to-all | bytes 589824 | tf_op jit(solution)/shard_map/all_to_all | solution.py:161
  52.1 10.9 %all_to_all.11 = f32[8,72,128]{2,1,0:T(8,128)} all-to-all(f32[8,72,128]{2,1,0:T(8,128)S(1)} %broadcast_in_dim.31), channel_id=1, replica_groups=mesh['mem'=8,'gx'=4,'gy'=16] {'mem'}, dimensions={0} | all-to-all | bytes 589824 | tf_op jit(solution)/shard_map/all_to_all | solution.py:163
  63.0 2.4 %back.1 = (f32[24,32,128]{2,1,0:T(8,128)}, f32[32,128]{1,0:T(8,128)}, f32[32,128]{1,0:T(8,128)}) custom-call(f32[18,32,128]{2,1,0:T(8,128)} %bitcast.24, s32[3,32,128]{2,1,0:T(8,128)} %refs_1_.3, f32[6]{0:T(128)} %refs_2_.1, bf16[8,6,3,32,128]{4,3,2,1,0:T(8,128)(2,1)} %refs_3_.1), custom_call_target="tpu_custom_call" | custom-call | tf_op jit(solution)/shard_map/back/pallas_call | solution.py:166
  65.4 7.9 %collective-permute-start.4 = (f32[32,128]{1,0:T(8,128)}, f32[32,128]{1,0:T(8,128)S(1)}, u32[]{:S(2)}, u32[]{:S(2)}) collective-permute-start(f32[32,128]{1,0:T(8,128)} %get-tuple-element.17), channel_id=1, source_target_pairs={{0,16},{16,32},{32,48},{1,17},{17,33},{33,49},{2,18},{18,34},{34,5... | collective-permute-start | bytes 49160 | tf_op jit(solution)/shard_map/ppermute | solution.py:18
  73.4 1.3 %collective-permute-start.5 = (f32[32,128]{1,0:T(8,128)}, f32[32,128]{1,0:T(8,128)S(1)}, u32[]{:S(2)}, u32[]{:S(2)}) collective-permute-start(f32[32,128]{1,0:T(8,128)} %get-tuple-element.18), channel_id=1, source_target_pairs={{16,0},{32,16},{48,32},{17,1},{33,17},{49,33},{18,2},{34,18},{50,3... | collective-permute-start | bytes 49160 | tf_op jit(solution)/shard_map/ppermute | solution.py:18
  74.7 1.0 fusion
  75.6 0.0 collective-permute-done.4.refs_3_
  75.6 0.0 copy-start.2
  75.7 7.5 %collective-permute-done.5.refs_4_ = f32[32,128]{1,0:T(8,128)S(1)} collective-permute-done((f32[32,128]{1,0:T(8,128)}, f32[32,128]{1,0:T(8,128)S(1)}, u32[]{:S(2)}, u32[]{:S(2)}) %collective-permute-start.5) | collective-permute-done | bytes 16416 | tf_op jit(solution)/shard_map/ppermute | solution.py:18
  83.1 1.9 %collective-permute-start.7 = (f32[26,4,128]{2,1,0:T(4,128)S(1)}, f32[26,4,128]{2,1,0:T(4,128)S(1)}, u32[]{:S(2)}, u32[]{:S(2)}) collective-permute-start(f32[26,4,128]{2,1,0:T(4,128)S(1)} %pad_maximum_fusion.5), channel_id=1, source_target_pairs={{0,1},{1,2},{2,3},{3,4},{4,5},{5,6},{6,7},{7,8},{8,9},{9,10},{10,1... | collective-permute-start | bytes 159752 | tf_op jit(solution)/shard_map/ppermute | solution.py:18
  85.1 3.9 %collective-permute-start.6 = (f32[26,4,128]{2,1,0:T(4,128)S(1)}, f32[26,4,128]{2,1,0:T(4,128)S(1)}, u32[]{:S(2)}, u32[]{:S(2)}) collective-permute-start(f32[26,4,128]{2,1,0:T(4,128)S(1)} %pad_maximum_fusion.4), channel_id=1, source_target_pairs={{1,0},{2,1},{3,2},{4,3},{5,4},{6,5},{7,6},{8,7},{9,8},{10,9},{11,1... | collective-permute-start | bytes 159752 | tf_op jit(solution)/shard_map/ppermute | solution.py:18
  89.0 0.1 collective-permute-done.7
  89.2 4.1 %collective-permute-done.6 = f32[26,4,128]{2,1,0:T(4,128)S(1)} collective-permute-done((f32[26,4,128]{2,1,0:T(4,128)S(1)}, f32[26,4,128]{2,1,0:T(4,128)S(1)}, u32[]{:S(2)}, u32[]{:S(2)}) %collective-permute-start.6) | collective-permute-done | bytes 53280 | tf_op jit(solution)/shard_map/ppermute | solution.py:18
  93.2 0.7 pad_maximum_fusion.1.refs_5_
  93.9 0.0 copy-done.2
  93.9 0.0 copy-done.3
  93.9 5.8 %adjoint.1 = f32[24,32,128]{2,1,0:T(8,128)} custom-call(f32[24,32,128]{2,1,0:T(8,128)} %bitcast.23, f32[24,32,128]{2,1,0:T(8,128)} %get-tuple-element.15.refs_1_, f32[3,40,256]{2,1,0:T(8,128)} %get-tuple-element.16.refs_2_, f32[32,128]{1,0:T(8,128)} %copy-done.2, f32[32,128]{1,0:T(8,128)} %copy-done.3, f32[26,8,128]{2,1,0:T(8,128)} %pad_maximum_fusion.1.refs_5_), custom_call_target="tpu_custom_call" | custom-call | tf_op jit(solution)/shard_map/adjoint/pallas_call | solution.py:181
  (13 shorter events, 0.1 us)
Async XLA Ops:
  1.9 12.1 %collective-permute-start = (f32[32,128]{1,0:T(8,128)}, f32[32,128]{1,0:T(8,128)S(1)}, u32[]{:S(2)}, u32[]{:S(2)}) collective-permute-start(f32[32,128]{1,0:T(8,128)} %get-tuple-element.12), channel_id=1, source_target_pairs={{0,16},{16,32},{32,48},{1,17},{17,33},{33,49},{2,18},{18,34},{34,5... | collective-permute-start | bytes 49160 | tf_op jit(solution)/shard_map/ppermute | solution.py:18
  11.0 11.2 %collective-permute-start.1 = (f32[32,128]{1,0:T(8,128)}, f32[32,128]{1,0:T(8,128)S(1)}, u32[]{:S(2)}, u32[]{:S(2)}) collective-permute-start(f32[32,128]{1,0:T(8,128)} %get-tuple-element.13), channel_id=1, source_target_pairs={{16,0},{32,16},{48,32},{17,1},{33,17},{49,33},{18,2},{34,18},{50,3... | collective-permute-start | bytes 49160 | tf_op jit(solution)/shard_map/ppermute | solution.py:18
  14.0 19.6 %copy-start = (f32[32,128]{1,0:T(8,128)}, f32[32,128]{1,0:T(8,128)S(1)}, u32[]{:S(2)}) copy-start(f32[32,128]{1,0:T(8,128)S(1)} %collective-permute-done.refs_2_) | copy-start | bytes 49156
  22.2 11.4 %copy-start.1 = (f32[32,128]{1,0:T(8,128)}, f32[32,128]{1,0:T(8,128)S(1)}, u32[]{:S(2)}) copy-start(f32[32,128]{1,0:T(8,128)S(1)} %collective-permute-done.1.refs_3_) | copy-start | bytes 49156
  22.2 6.1 %collective-permute-start.3 = (f32[29,4,128]{2,1,0:T(4,128)S(1)}, f32[29,4,128]{2,1,0:T(4,128)S(1)}, u32[]{:S(2)}, u32[]{:S(2)}) collective-permute-start(f32[29,4,128]{2,1,0:T(4,128)S(1)} %pad_maximum_fusion.3), channel_id=1, source_target_pairs={{0,1},{1,2},{2,3},{3,4},{4,5},{5,6},{6,7},{7,8},{8,9},{9,10},{10,1... | collective-permute-start | bytes 178184 | tf_op jit(solution)/shard_map/ppermute | solution.py:18
  24.6 8.2 %collective-permute-start.2 = (f32[29,4,128]{2,1,0:T(4,128)S(1)}, f32[29,4,128]{2,1,0:T(4,128)S(1)}, u32[]{:S(2)}, u32[]{:S(2)}) collective-permute-start(f32[29,4,128]{2,1,0:T(4,128)S(1)} %pad_maximum_fusion.2), channel_id=1, source_target_pairs={{1,0},{2,1},{3,2},{4,3},{5,4},{6,5},{7,6},{8,7},{9,8},{10,9},{11,1... | collective-permute-start | bytes 178184 | tf_op jit(solution)/shard_map/ppermute | solution.py:18
  65.4 10.2 %collective-permute-start.4 = (f32[32,128]{1,0:T(8,128)}, f32[32,128]{1,0:T(8,128)S(1)}, u32[]{:S(2)}, u32[]{:S(2)}) collective-permute-start(f32[32,128]{1,0:T(8,128)} %get-tuple-element.17), channel_id=1, source_target_pairs={{0,16},{16,32},{32,48},{1,17},{17,33},{33,49},{2,18},{18,34},{34,5... | collective-permute-start | bytes 49160 | tf_op jit(solution)/shard_map/ppermute | solution.py:18
  73.4 9.8 %collective-permute-start.5 = (f32[32,128]{1,0:T(8,128)}, f32[32,128]{1,0:T(8,128)S(1)}, u32[]{:S(2)}, u32[]{:S(2)}) collective-permute-start(f32[32,128]{1,0:T(8,128)} %get-tuple-element.18), channel_id=1, source_target_pairs={{16,0},{32,16},{48,32},{17,1},{33,17},{49,33},{18,2},{34,18},{50,3... | collective-permute-start | bytes 49160 | tf_op jit(solution)/shard_map/ppermute | solution.py:18
  75.6 18.2 %copy-start.2 = (f32[32,128]{1,0:T(8,128)}, f32[32,128]{1,0:T(8,128)S(1)}, u32[]{:S(2)}) copy-start(f32[32,128]{1,0:T(8,128)S(1)} %collective-permute-done.4.refs_3_) | copy-start | bytes 49156
  83.1 10.8 %copy-start.3 = (f32[32,128]{1,0:T(8,128)}, f32[32,128]{1,0:T(8,128)S(1)}, u32[]{:S(2)}) copy-start(f32[32,128]{1,0:T(8,128)S(1)} %collective-permute-done.5.refs_4_) | copy-start | bytes 49156
  83.1 6.0 %collective-permute-start.7 = (f32[26,4,128]{2,1,0:T(4,128)S(1)}, f32[26,4,128]{2,1,0:T(4,128)S(1)}, u32[]{:S(2)}, u32[]{:S(2)}) collective-permute-start(f32[26,4,128]{2,1,0:T(4,128)S(1)} %pad_maximum_fusion.5), channel_id=1, source_target_pairs={{0,1},{1,2},{2,3},{3,4},{4,5},{5,6},{6,7},{7,8},{8,9},{9,10},{10,1... | collective-permute-start | bytes 159752 | tf_op jit(solution)/shard_map/ppermute | solution.py:18
  85.1 8.1 %collective-permute-start.6 = (f32[26,4,128]{2,1,0:T(4,128)S(1)}, f32[26,4,128]{2,1,0:T(4,128)S(1)}, u32[]{:S(2)}, u32[]{:S(2)}) collective-permute-start(f32[26,4,128]{2,1,0:T(4,128)S(1)} %pad_maximum_fusion.4), channel_id=1, source_target_pairs={{1,0},{2,1},{3,2},{4,3},{5,4},{6,5},{7,6},{8,7},{9,8},{10,9},{11,1... | collective-permute-start | bytes 159752 | tf_op jit(solution)/shard_map/ppermute | solution.py:18

commit v2 on v1

v2 whole, which is shorter than its diff:
```python
import math

import jax
import jax.numpy as jnp
from jax import lax
from jax.experimental import pallas as pl
from jax.experimental.pallas import tpu as pltpu
from jax.sharding import PartitionSpec as P

STEPS = 4
LANES = 128
PARAMS = pltpu.CompilerParams(vmem_limit_bytes=16 << 20)


def swap(near, far, axis):
    size = lax.axis_size(axis)
    out = []
    for value, start in ((near, 0), (far, 1)):
        pairs = []
        for i in range(start, size - 1, 2):
            pairs += [(i, i + 1), (i + 1, i)]
        out.append(lax.ppermute(value, axis, pairs))
    return out


def is_odd(axis):
    return lax.rem(lax.axis_index(axis), 2) == 1


def ordered(odd, first, last):
    return jnp.where(odd, first, last), jnp.where(odd, last, first)


def lane_ids(rows):
    return lax.broadcasted_iota(jnp.int32, (rows, LANES), 1)


def send_rows(count, source, near, far):
    odd = is_odd("gy")
    for p in range(count):
        plane = source(p)
        rows = plane.shape[0]
        near[p], far[p] = ordered(odd, plane[:STEPS], plane[rows - STEPS :])


def rows_kernel(control, diffusivity, near, far):
    count = control.shape[0]
    levels = diffusivity.shape[0]
    send_rows(count + levels, lambda p: control[p] if p < count else diffusivity[p - count], near, far)


def columns_kernel(parts, *refs):
    arrays, (got_near, got_far, rim, near, far) = refs[:parts], refs[parts:]
    odd = is_odd("gy")
    planes = [(a, p) for a in arrays for p in range(a.shape[0])]
    rows = arrays[0].shape[1] + 2 * STEPS
    group = lane_ids(rows) // STEPS
    first = jnp.zeros((rows, LANES), jnp.float32)
    last = jnp.zeros((rows, LANES), jnp.float32)
    for p, (a, q) in enumerate(planes):
        after, before = ordered(odd, got_far[p], got_near[p])
        ring = jnp.concatenate([after, before], axis=0)
        rim[p] = ring
        plane = jnp.concatenate([a[q], ring], axis=0)
        first = jnp.where(group == p, pltpu.roll(plane, (STEPS * p) % LANES, 1), first)
        last = jnp.where(group == p, pltpu.roll(plane, (STEPS * p + STEPS) % LANES, 1), last)
    near[...], far[...] = ordered(is_odd("gx"), first, last)


def sides_of(near, far):
    east, west = ordered(is_odd("gx"), far[...], near[...])
    return west, east


def widened(main, rim, west, east, p):
    lane = lane_ids(west.shape[0])
    east_part = pltpu.roll(east, lax.rem(2 * LANES - STEPS * p, LANES), 1)
    west_part = pltpu.roll(west, lax.rem(2 * LANES - STEPS - STEPS * p, LANES), 1)
    side = jnp.where(lane < STEPS, east_part, jnp.where(lane >= LANES - STEPS, west_part, 0.0))
    return jnp.concatenate([jnp.concatenate([main, rim], axis=0), side], axis=1)


def neighbours(field):
    rows, lanes = field.shape
    return (
        pltpu.roll(field, 1, 0)
        + pltpu.roll(field, rows - 1, 0)
        + pltpu.roll(field, 1, 1)
        + pltpu.roll(field, lanes - 1, 1)
    )


def spread_kernel(control, diffusivity, rim, near, far, perturb_hbm, partial, wide_diff, spread, perturb, sem):
    copy = pltpu.make_async_copy(perturb_hbm, perturb, sem)
    copy.start()
    count, rows, _ = control.shape
    levels = diffusivity.shape[0]
    members = count // levels
    variables = perturb.shape[1]
    west, east = sides_of(near, far)
    for l in range(levels):
        wide_diff[l] = widened(diffusivity[l], rim[count + l], west, east, count + l)

    def one(m, carry):
        for l in range(levels):
            p = m * levels + l
            field = widened(control[p], rim[p], west, east, p)
            for _ in range(STEPS):
                field = field + wide_diff[l] * (neighbours(field) - 4.0 * field)
            spread[p] = field[:rows, :LANES]
        return carry

    lax.fori_loop(0, members, one, 0)
    copy.wait()
    for v in range(variables):
        for l in range(levels):
            total = perturb[0, v, l].astype(jnp.float32) * spread[l]
            for m in range(1, members):
                total = total + perturb[m, v, l].astype(jnp.float32) * spread[m * levels + l]
            partial[v * levels + l] = total


def back_kernel(scale, increment, obs_count, obs_weight, perturb, back, near, far, weighted):
    members, variables, levels, rows, _ = perturb.shape
    for l in range(levels):
        seen = obs_count[l].astype(jnp.float32) * (scale * scale)
        for v in range(variables):
            weighted[v * levels + l] = seen * obs_weight[v] * increment[v * levels + l]
    for m in range(members):
        for l in range(levels):
            total = perturb[m, 0, l].astype(jnp.float32) * weighted[l]
            for v in range(1, variables):
                total = total + perturb[m, v, l].astype(jnp.float32) * weighted[v * levels + l]
            back[m * levels + l] = total
    send_rows(members * levels, lambda p: back[p], near, far)


def adjoint_kernel(control, back, wide_diff, rim, near, far, out):
    count, rows, _ = back.shape
    levels = wide_diff.shape[0]
    west, east = sides_of(near, far)

    def one(m, carry):
        for l in range(levels):
            p = m * levels + l
            field = widened(back[p], rim[p], west, east, p)
            for _ in range(STEPS):
                carried = wide_diff[l] * field
                field = field + (neighbours(carried) - 4.0 * carried)
            out[p] = control[p] + field[:rows, :LANES]
        return carry

    lax.fori_loop(0, count // levels, one, 0)


def shape_of(*shape):
    return jax.ShapeDtypeStruct(shape, jnp.float32)


def columns(*arrays, rows):
    total = sum(a.shape[0] for a in arrays)
    ring = arrays[0].shape[1] + 2 * STEPS
    near, far = rows
    rim, near, far = pl.pallas_call(
        lambda *refs: columns_kernel(len(arrays), *refs),
        out_shape=(shape_of(total, 2 * STEPS, LANES), shape_of(ring, LANES), shape_of(ring, LANES)),
        compiler_params=PARAMS,
        name="columns",
    )(*arrays, near, far)
    return rim, *swap(near, far, "gx")


def shards(control, perturb, obs_count, obs_weight, diffusivity):
    members, levels, rows, lanes = control.shape
    variables = perturb.shape[1]
    ways = lax.axis_size("mem")
    scale = 1.0 / math.sqrt(members * ways - 1)
    count = members * levels
    ring = rows + 2 * STEPS
    flat = control.reshape(count, rows, lanes)
    vmem = pl.BlockSpec(memory_space=pltpu.VMEM)

    edge = shape_of(count + levels, STEPS, lanes)
    near, far = pl.pallas_call(rows_kernel, out_shape=(edge, edge), compiler_params=PARAMS, name="rows")(flat, diffusivity)
    rim, near, far = columns(flat, diffusivity, rows=swap(near, far, "gy"))

    partial, wide_diff = pl.pallas_call(
        spread_kernel,
        out_shape=(shape_of(variables * levels, rows, lanes), shape_of(levels, ring, 2 * lanes)),
        in_specs=[vmem] * 5 + [pl.BlockSpec(memory_space=pltpu.HBM)],
        scratch_shapes=[
            pltpu.VMEM((count, rows, lanes), jnp.float32),
            pltpu.VMEM(perturb.shape, perturb.dtype),
            pltpu.SemaphoreType.DMA,
        ],
        compiler_params=PARAMS,
        name="spread",
    )(flat, diffusivity, rim, near, far, pltpu.with_memory_space_constraint(perturb, pltpu.HBM))

    parts = lax.all_to_all(partial.reshape(ways, -1, lanes), "mem", 0, 0)
    mine = jnp.sum(parts, axis=0)
    increment = lax.all_to_all(jnp.broadcast_to(mine, parts.shape), "mem", 0, 0)
    increment = increment.reshape(variables * levels, rows, lanes)

    edge = shape_of(count, STEPS, lanes)
    back, near, far = pl.pallas_call(
        lambda *refs: back_kernel(scale, *refs),
        out_shape=(shape_of(count, rows, lanes), edge, edge),
        in_specs=[vmem, vmem, pl.BlockSpec(memory_space=pltpu.SMEM), vmem],
        scratch_shapes=[pltpu.VMEM((variables * levels, rows, lanes), jnp.float32)],
        compiler_params=PARAMS,
        name="back",
    )(increment, obs_count, obs_weight, perturb)
    rim, near, far = columns(back, rows=swap(near, far, "gy"))

    out = pl.pallas_call(adjoint_kernel, out_shape=shape_of(count, rows, lanes), compiler_params=PARAMS, name="adjoint")(
        flat, back, wide_diff, rim, near, far
    )
    return out.reshape(control.shape)


def solution(mesh):
    placed = (
        P("mem", None, "gy", "gx"),
        P("mem", None, None, "gy", "gx"),
        P(None, "gy", "gx"),
        P(),
        P(None, "gy", "gx"),
    )
    return jax.shard_map(
        shards, mesh=mesh, in_specs=placed, out_specs=P("mem", None, "gy", "gx"), check_vma=False
    )
```

time: 100 us -> 82.6 us (0.83)
  waiting for transfers between devices: 24.6 us -> 9.74 us
  Pallas kernels: 16.5 us -> 10.3 us
  starting transfers between devices: 31.3 us -> 37 us
  other arithmetic: 1.42 us -> 0.02 us
    ppermute x8, waiting for transfers between devices: 24.6 us -> 9.74 us  [swap(): out.append(lax.ppermute(value, axis, pairs))]
    ppermute x8, starting transfers between devices: 31.3 us -> 37 us  [swap(): out.append(lax.ppermute(value, axis, pairs))]
    pallas_call x3 -> x5, Pallas kernels: 14.1 us -> 9.46 us  [the longest x1 4.63 us: shards(): pl.pallas_call(adjoint_kernel, out_shape=shape_of(count, rows, lanes), co...]
    slice x3 -> x0, local copies, waits for them, and re-layouts: 2.65 us -> none  [rim_rows(): p[:, :STEPS]]
    unnamed x8 -> x12, local copies, waits for them, and re-layouts: 0.02 us -> 1.82 us
    pallas_call x1, Pallas kernels: 2.41 us -> 0.8 us  [shards(): pl.pallas_call(lambda *refs: back_kernel(scale, *refs), out_shape=(shape_...]
    concatenate x6 -> x0, other arithmetic: 1.4 us -> none  [the longest x2 1.34 us: rim_rows(): return jnp.concatenate([from_south, from_north], axis=1)]
  transfers between devices with their start and end apart: 8 -> 8, of which waited for: 6 -> 4; matrix products, arithmetic and copies ran while one was open for 3% -> 0% of each run, Pallas kernels for 0% -> 0%
where the time goes in v2:
time: 82.6 us; the launch traced here: 81.5 us
  starting transfers between devices  37 us (45%)
  blocking collectives  22.4 us (27%)
  Pallas kernels  10.3 us (12%)
  waiting for transfers between devices  9.74 us (12%)
  local copies, waits for them, and re-layouts  1.84 us (2%)
    ppermute x8, starting transfers between devices, swap(): out.append(lax.ppermute(value, axis, pairs))  37 us
    all_to_all x1, blocking collectives, shards(): parts = lax.all_to_all(partial.reshape(ways, -1, lanes), 'mem', 0, 0)  12.1 us
    all_to_all x1, blocking collectives, shards(): increment = lax.all_to_all(jnp.broadcast_to(mine, parts.shape), 'mem', 0, 0)  10.4 us
    ppermute x8, waiting for transfers between devices, swap(): out.append(lax.ppermute(value, axis, pairs))  9.74 us
    pallas_call x1, Pallas kernels, shards(): pl.pallas_call(adjoint_kernel, out_shape=shape_of(count, rows, lanes), co...  4.63 us
    pallas_call x1, Pallas kernels, shards(): pl.pallas_call(spread_kernel, out_shape=(shape_of(variables * levels, row...  4.14 us
    unnamed x12, local copies, waits for them, and re-layouts  1.82 us
  transfers between devices with their start and end apart: 8, of which 4 were waited for; matrix products, arithmetic and copies ran while one was open for 0% of the time, Pallas kernels for 0%

profile of v2, /device:TPU:24, one launch (start us, length us, event | category | flops | bytes accessed | tf_op | source)
XLA Modules:
  0.0 81.5 jit_solution(10649719468674746921)
XLA Ops:
  0.0 1.0 %copy-done = f32[8,3,32,128]{3,2,1,0:T(8,128)S(1)} copy-done((f32[8,3,32,128]{3,2,1,0:T(8,128)S(1)}, f32[8,3,32,128]{3,2,1,0:T(8,128)}, u32[]{:S(2)}) %copy-start) | copy-done | bytes 393240
  1.0 0.8 copy-done.3
  1.8 2.7 %collective-permute-start = (f32[27,4,128]{2,1,0:T(4,128)S(1)}, f32[27,4,128]{2,1,0:T(4,128)S(1)}, u32[]{:S(2)}, u32[]{:S(2)}) collective-permute-start(f32[27,4,128]{2,1,0:T(4,128)S(1)} %get-tuple-element.18), channel_id=1, source_target_pairs={{0,1},{1,0},{2,3},{3,2},{4,5},{5,4},{6,7},{7,6},{8,9},{9,8},{10,11... | collective-permute-start | bytes 165896 | tf_op jit(solution)/shard_map/ppermute | solution.py:22
  4.5 4.3 %collective-permute-start.1 = (f32[27,4,128]{2,1,0:T(4,128)S(1)}, f32[27,4,128]{2,1,0:T(4,128)S(1)}, u32[]{:S(2)}, u32[]{:S(2)}) collective-permute-start(f32[27,4,128]{2,1,0:T(4,128)S(1)} %get-tuple-element.19), channel_id=1, source_target_pairs={{1,2},{2,1},{3,4},{4,3},{5,6},{6,5},{7,8},{8,7},{9,10},{10,9},{11,... | collective-permute-start | bytes 165896 | tf_op jit(solution)/shard_map/ppermute | solution.py:22
  8.8 0.0 collective-permute-done.refs_2_
  8.8 3.8 %collective-permute-done.1.refs_3_ = f32[27,4,128]{2,1,0:T(4,128)S(1)} collective-permute-done((f32[27,4,128]{2,1,0:T(4,128)S(1)}, f32[27,4,128]{2,1,0:T(4,128)S(1)}, u32[]{:S(2)}, u32[]{:S(2)}) %collective-permute-start.1) | collective-permute-done | bytes 55328 | tf_op jit(solution)/shard_map/ppermute | solution.py:22
  12.6 0.3 columns.2
  13.0 9.1 %collective-permute-start.2 = (f32[40,128]{1,0:T(8,128)S(1)}, f32[40,128]{1,0:T(8,128)S(1)}, u32[]{:S(2)}, u32[]{:S(2)}) collective-permute-start(f32[40,128]{1,0:T(8,128)S(1)} %get-tuple-element.21), channel_id=1, source_target_pairs={{0,16},{16,0},{32,48},{48,32},{1,17},{17,1},{33,49},{49,33},{2,18}... | collective-permute-start | bytes 61448 | tf_op jit(solution)/shard_map/ppermute | solution.py:22
  22.1 0.7 collective-permute-start.3
  22.8 1.1 %collective-permute-done.2.near = f32[40,128]{1,0:T(8,128)S(1)} collective-permute-done((f32[40,128]{1,0:T(8,128)S(1)}, f32[40,128]{1,0:T(8,128)S(1)}, u32[]{:S(2)}, u32[]{:S(2)}) %collective-permute-start.2) | collective-permute-done | bytes 20512 | tf_op jit(solution)/shard_map/ppermute | solution.py:22
  23.9 0.0 collective-permute-done.3.far
  23.9 4.1 %spread.1 = (f32[18,32,128]{2,1,0:T(8,128)S(1)}, f32[3,40,256]{2,1,0:T(8,128)S(1)}) custom-call(f32[24,32,128]{2,1,0:T(8,128)S(1)} %bitcast.6, f32[3,32,128]{2,1,0:T(8,128)S(1)} %copy-done.3, f32[27,8,128]{2,1,0:T(8,128)S(1)} %get-tuple-element.20.rim, f32[40,128]{1,0:T(8,128)S(1)} %collective-permute-done.2.near, f32[40,128]{1,0:T(8,128)S(1)} %collective-permute-done.3.far, ...), custom_call_target="tpu_custom_call" | custom-call | tf_op jit(solution)/shard_map/spread/pallas_call | solution.py:187
  28.0 0.0 copy-start.2
  28.0 0.0 copy-start.4
  28.0 0.0 copy-start.5
  28.0 12.1 %all_to_all.10 = f32[8,72,128]{2,1,0:T(8,128)S(1)} all-to-all(f32[8,72,128]{2,1,0:T(8,128)S(1)} %bitcast.9), channel_id=1, replica_groups=mesh['mem'=8,'gx'=4,'gy'=16] {'mem'}, dimensions={0} | all-to-all | bytes 589824 | tf_op jit(solution)/shard_map/all_to_all | solution.py:200
  40.2 0.0 copy-start.1
  40.2 10.4 %all_to_all.11 = f32[8,72,128]{2,1,0:T(8,128)S(1)} all-to-all(f32[8,72,128]{2,1,0:T(8,128)S(1)} %broadcast_in_dim.3), channel_id=1, replica_groups=mesh['mem'=8,'gx'=4,'gy'=16] {'mem'}, dimensions={0} | all-to-all | bytes 589824 | tf_op jit(solution)/shard_map/all_to_all | solution.py:202
  50.6 0.0 copy-done.2
  50.6 0.0 copy-done.4
  50.6 0.0 copy-done.5
  50.6 0.8 back.1
  51.4 1.9 %collective-permute-start.4 = (f32[24,4,128]{2,1,0:T(4,128)S(1)}, f32[24,4,128]{2,1,0:T(4,128)S(1)}, u32[]{:S(2)}, u32[]{:S(2)}) collective-permute-start(f32[24,4,128]{2,1,0:T(4,128)S(1)} %get-tuple-element.26), channel_id=1, source_target_pairs={{0,1},{1,0},{2,3},{3,2},{4,5},{5,4},{6,7},{7,6},{8,9},{9,8},{10,11... | collective-permute-start | bytes 147464 | tf_op jit(solution)/shard_map/ppermute | solution.py:22
  53.3 4.3 %collective-permute-start.5 = (f32[24,4,128]{2,1,0:T(4,128)S(1)}, f32[24,4,128]{2,1,0:T(4,128)S(1)}, u32[]{:S(2)}, u32[]{:S(2)}) collective-permute-start(f32[24,4,128]{2,1,0:T(4,128)S(1)} %get-tuple-element.27), channel_id=1, source_target_pairs={{1,2},{2,1},{3,4},{4,3},{5,6},{6,5},{7,8},{8,7},{9,10},{10,9},{11,... | collective-permute-start | bytes 147464 | tf_op jit(solution)/shard_map/ppermute | solution.py:22
  57.6 0.0 collective-permute-done.4.refs_1_
  57.6 3.8 %collective-permute-done.5.refs_2_ = f32[24,4,128]{2,1,0:T(4,128)S(1)} collective-permute-done((f32[24,4,128]{2,1,0:T(4,128)S(1)}, f32[24,4,128]{2,1,0:T(4,128)S(1)}, u32[]{:S(2)}, u32[]{:S(2)}) %collective-permute-start.5) | collective-permute-done | bytes 49184 | tf_op jit(solution)/shard_map/ppermute | solution.py:22
  61.4 0.3 columns.3
  61.7 13.4 %collective-permute-start.6 = (f32[40,128]{1,0:T(8,128)S(1)}, f32[40,128]{1,0:T(8,128)S(1)}, u32[]{:S(2)}, u32[]{:S(2)}) collective-permute-start(f32[40,128]{1,0:T(8,128)S(1)} %get-tuple-element.29), channel_id=1, source_target_pairs={{0,16},{16,0},{32,48},{48,32},{1,17},{17,1},{33,49},{49,33},{2,18}... | collective-permute-start | bytes 61448 | tf_op jit(solution)/shard_map/ppermute | solution.py:22
  75.1 0.7 collective-permute-start.7
  75.8 1.1 %collective-permute-done.6.near = f32[40,128]{1,0:T(8,128)S(1)} collective-permute-done((f32[40,128]{1,0:T(8,128)S(1)}, f32[40,128]{1,0:T(8,128)S(1)}, u32[]{:S(2)}, u32[]{:S(2)}) %collective-permute-start.6) | collective-permute-done | bytes 20512 | tf_op jit(solution)/shard_map/ppermute | solution.py:22
  76.9 0.0 collective-permute-done.7.far
  76.9 4.6 %adjoint.1 = f32[24,32,128]{2,1,0:T(8,128)} custom-call(f32[24,32,128]{2,1,0:T(8,128)S(1)} %bitcast.7, f32[24,32,128]{2,1,0:T(8,128)S(1)} %get-tuple-element.24.refs_0_.back, f32[3,40,256]{2,1,0:T(8,128)S(1)} %get-tuple-element.25.wide_diff, f32[24,8,128]{2,1,0:T(8,128)S(1)} %get-tuple-element.28.rim, f32[40,128]{1,0:T(8,128)S(1)} %collective-permute-done.6.near, ...), custom_call_target="tpu_custom_call" | custom-call | tf_op jit(solution)/shard_map/adjoint/pallas_call | solution.py:216
  (6 shorter events, 0.1 us)
Async XLA Ops:
  0.0 1.0 %copy-start = (f32[8,3,32,128]{3,2,1,0:T(8,128)S(1)}, f32[8,3,32,128]{3,2,1,0:T(8,128)}, u32[]{:S(2)}) copy-start(f32[8,3,32,128]{3,2,1,0:T(8,128)} %param.5) | copy-start | bytes 1179652
  1.0 0.8 copy-start.3
  1.8 7.0 %collective-permute-start = (f32[27,4,128]{2,1,0:T(4,128)S(1)}, f32[27,4,128]{2,1,0:T(4,128)S(1)}, u32[]{:S(2)}, u32[]{:S(2)}) collective-permute-start(f32[27,4,128]{2,1,0:T(4,128)S(1)} %get-tuple-element.18), channel_id=1, source_target_pairs={{0,1},{1,0},{2,3},{3,2},{4,5},{5,4},{6,7},{7,6},{8,9},{9,8},{10,11... | collective-permute-start | bytes 165896 | tf_op jit(solution)/shard_map/ppermute | solution.py:22
  4.5 8.2 %collective-permute-start.1 = (f32[27,4,128]{2,1,0:T(4,128)S(1)}, f32[27,4,128]{2,1,0:T(4,128)S(1)}, u32[]{:S(2)}, u32[]{:S(2)}) collective-permute-start(f32[27,4,128]{2,1,0:T(4,128)S(1)} %get-tuple-element.19), channel_id=1, source_target_pairs={{1,2},{2,1},{3,4},{4,3},{5,6},{6,5},{7,8},{8,7},{9,10},{10,9},{11,... | collective-permute-start | bytes 165896 | tf_op jit(solution)/shard_map/ppermute | solution.py:22
  13.0 10.9 %collective-permute-start.2 = (f32[40,128]{1,0:T(8,128)S(1)}, f32[40,128]{1,0:T(8,128)S(1)}, u32[]{:S(2)}, u32[]{:S(2)}) collective-permute-start(f32[40,128]{1,0:T(8,128)S(1)} %get-tuple-element.21), channel_id=1, source_target_pairs={{0,16},{16,0},{32,48},{48,32},{1,17},{17,1},{33,49},{49,33},{2,18}... | collective-permute-start | bytes 61448 | tf_op jit(solution)/shard_map/ppermute | solution.py:22
  22.1 1.7 %collective-permute-start.3 = (f32[40,128]{1,0:T(8,128)S(1)}, f32[40,128]{1,0:T(8,128)S(1)}, u32[]{:S(2)}, u32[]{:S(2)}) collective-permute-start(f32[40,128]{1,0:T(8,128)S(1)} %get-tuple-element.22), channel_id=1, source_target_pairs={{16,32},{32,16},{17,33},{33,17},{18,34},{34,18},{19,35},{35,19},{2... | collective-permute-start | bytes 61448 | tf_op jit(solution)/shard_map/ppermute | solution.py:22
  28.0 22.6 %copy-start.2 = (bf16[8,6,3,32,128]{4,3,2,1,0:T(8,128)(2,1)S(1)}, bf16[8,6,3,32,128]{4,3,2,1,0:T(8,128)(2,1)}, u32[]{:S(2)}) copy-start(bf16[8,6,3,32,128]{4,3,2,1,0:T(8,128)(2,1)} %refs_3_.1) | copy-start | bytes 3538948
  28.0 22.5 %copy-start.4 = (s32[3,32,128]{2,1,0:T(8,128)S(1)}, s32[3,32,128]{2,1,0:T(8,128)}, u32[]{:S(2)}) copy-start(s32[3,32,128]{2,1,0:T(8,128)} %refs_1_.3) | copy-start | bytes 147460
  28.0 22.5 %copy-start.5 = (f32[6]{0:T(128)S(1)}, f32[6]{0:T(128)}, u32[]{:S(2)}) copy-start(f32[6]{0:T(128)} %refs_2_.1) | copy-start | bytes 76
  40.2 36.7 %copy-start.1 = (f32[8,3,32,128]{3,2,1,0:T(8,128)S(1)}, f32[8,3,32,128]{3,2,1,0:T(8,128)}, u32[]{:S(2)}) copy-start(f32[8,3,32,128]{3,2,1,0:T(8,128)} %param.5) | copy-start | bytes 1179652
  51.4 6.3 %collective-permute-start.4 = (f32[24,4,128]{2,1,0:T(4,128)S(1)}, f32[24,4,128]{2,1,0:T(4,128)S(1)}, u32[]{:S(2)}, u32[]{:S(2)}) collective-permute-start(f32[24,4,128]{2,1,0:T(4,128)S(1)} %get-tuple-element.26), channel_id=1, source_target_pairs={{0,1},{1,0},{2,3},{3,2},{4,5},{5,4},{6,7},{7,6},{8,9},{9,8},{10,11... | collective-permute-start | bytes 147464 | tf_op jit(solution)/shard_map/ppermute | solution.py:22
  53.3 8.1 %collective-permute-start.5 = (f32[24,4,128]{2,1,0:T(4,128)S(1)}, f32[24,4,128]{2,1,0:T(4,128)S(1)}, u32[]{:S(2)}, u32[]{:S(2)}) collective-permute-start(f32[24,4,128]{2,1,0:T(4,128)S(1)} %get-tuple-element.27), channel_id=1, source_target_pairs={{1,2},{2,1},{3,4},{4,3},{5,6},{6,5},{7,8},{8,7},{9,10},{10,9},{11,... | collective-permute-start | bytes 147464 | tf_op jit(solution)/shard_map/ppermute | solution.py:22
  61.7 15.1 %collective-permute-start.6 = (f32[40,128]{1,0:T(8,128)S(1)}, f32[40,128]{1,0:T(8,128)S(1)}, u32[]{:S(2)}, u32[]{:S(2)}) collective-permute-start(f32[40,128]{1,0:T(8,128)S(1)} %get-tuple-element.29), channel_id=1, source_target_pairs={{0,16},{16,0},{32,48},{48,32},{1,17},{17,1},{33,49},{49,33},{2,18}... | collective-permute-start | bytes 61448 | tf_op jit(solution)/shard_map/ppermute | solution.py:22
  75.1 1.7 %collective-permute-start.7 = (f32[40,128]{1,0:T(8,128)S(1)}, f32[40,128]{1,0:T(8,128)S(1)}, u32[]{:S(2)}, u32[]{:S(2)}) collective-permute-start(f32[40,128]{1,0:T(8,128)S(1)} %get-tuple-element.30), channel_id=1, source_target_pairs={{16,32},{32,16},{17,33},{33,17},{18,34},{34,18},{19,35},{35,19},{2... | collective-permute-start | bytes 61448 | tf_op jit(solution)/shard_map/ppermute | solution.py:22

commit v3 on v0

v3 whole, which is shorter than its diff:
```python
import math

import jax
import jax.numpy as jnp
from jax import lax
from jax.experimental import pallas as pl
from jax.experimental.pallas import tpu as pltpu
from jax.sharding import PartitionSpec as P

STEPS = 4
LANES = 128
SUBLANES = 8
PARAMS = pltpu.CompilerParams(vmem_limit_bytes=16 << 20)


def swap(near, far, axis):
    size = lax.axis_size(axis)
    out = []
    for value, start in ((near, 0), (far, 1)):
        pairs = []
        for i in range(start, size - 1, 2):
            pairs += [(i, i + 1), (i + 1, i)]
        out.append(lax.ppermute(value, axis, pairs))
    return out


def is_odd(axis):
    return lax.rem(lax.axis_index(axis), 2) == 1


def ordered(odd, first, last):
    return jnp.where(odd, first, last), jnp.where(odd, last, first)


class Grid:
    def __init__(self, members, levels, rows):
        self.members, self.levels, self.rows = members, levels, rows
        self.ring = rows + 2 * STEPS
        self.block = LANES // levels // STEPS * STEPS
        self.per = self.block // STEPS
        self.packs = -(-self.ring // self.per)

    def members_at(self, level, y):
        return pl.ds(level * self.rows + y, self.members, stride=self.levels * self.rows)

    def ring_row(self, field, got, odd, level, k):
        y = k - STEPS
        if 0 <= y < self.rows:
            return field[self.members_at(level, y), :]
        before = y < 0
        at = level * STEPS + (k if before else y - self.rows)
        near, far = got
        after_value, before_value = ordered(odd, far[at], near[at])
        return before_value if before else after_value

    def lanes(self, rows=SUBLANES):
        lane = lax.broadcasted_iota(jnp.int32, (rows, LANES), 1)
        return lax.rem(lane, self.block)


def within(place, start, size):
    return (place >= start) & (place < start + size)


def rolled(value, shift):
    shift %= LANES
    return pltpu.roll(value, shift, 1) if shift else value


def edges_of(grid, value_of, rows=SUBLANES):
    lane = lax.broadcasted_iota(jnp.int32, (rows, LANES), 1)
    out = jnp.zeros((rows, LANES), jnp.float32)
    for l in range(grid.levels):
        base = l * grid.block
        out = jnp.where(within(lane, base, 4 * STEPS), rolled(value_of(l), base + 2 * STEPS), out)
    return out


def packed(grid, edges, rows=SUBLANES):
    place = grid.lanes(rows)
    first = jnp.zeros((rows, LANES), jnp.float32)
    last = first
    for i, value in enumerate(edges):
        mask = within(place, i * STEPS, STEPS)
        first = jnp.where(mask, rolled(value, (i - 2) * STEPS), first)
        last = jnp.where(mask, rolled(value, (i - 1) * STEPS), last)
    return first, last


def strip_of(grid, edges, west, east, i, rows=SUBLANES):
    place = grid.lanes(rows)
    out = jnp.where(place < 2 * STEPS, edges, 0.0)
    out = jnp.where(within(place, 6 * STEPS, 2 * STEPS), rolled(edges, 4 * STEPS), out)
    out = jnp.where(within(place, 2 * STEPS, STEPS), rolled(east, (2 - i) * STEPS), out)
    return jnp.where(within(place, 5 * STEPS, STEPS), rolled(west, (5 - i) * STEPS), out)


def joined(grid, strip):
    return jnp.where(grid.lanes() < 2 * STEPS, strip, rolled(strip, -4 * STEPS))


def merged(grid, main, ends, level):
    lane = lax.broadcasted_iota(jnp.int32, (SUBLANES, LANES), 1)
    outer = (lane < STEPS) | (lane >= LANES - STEPS)
    return jnp.where(outer, rolled(ends, LANES - 2 * STEPS - level * grid.block), main)


def lateral(value):
    return pltpu.roll(value, 1, 1) + pltpu.roll(value, LANES - 1, 1)


def spread_steps(field, coef, keep):
    for s in range(1, STEPS + 1):
        new = list(field)
        for k in range(s, len(field) - s):
            around = (field[k - 1] + field[k + 1]) + lateral(field[k])
            new[k] = keep(k) * field[k] + coef(k) * around
        field = new
    return field[STEPS:-STEPS]


def adjoint_steps(field, coef, keep):
    for s in range(1, STEPS + 1):
        flux = {k: coef(k) * field[k] for k in range(s - 1, len(field) - s + 1)}
        new = list(field)
        for k in range(s, len(field) - s):
            new[k] = keep(k) * field[k] + ((flux[k - 1] + flux[k + 1]) + lateral(flux[k]))
        field = new
    return field[STEPS:-STEPS]


def row_reader(ref, start):
    return lambda k: jnp.broadcast_to(ref[pl.ds(start + k, 1), :], (SUBLANES, LANES))


def rows_kernel(grid, control_hbm, diffusivity_hbm, near, far, control, diffusivity, sems):
    levels, rows = grid.levels, grid.rows
    copies = [
        pltpu.make_async_copy(diffusivity_hbm, diffusivity, sems.at[0]),
        pltpu.make_async_copy(control_hbm, control, sems.at[1]),
    ]
    for copy in copies:
        copy.start()
    odd = is_odd("gy")
    copies[0].wait()
    for l in range(levels):
        first = diffusivity[l * rows : l * rows + STEPS, :]
        last = diffusivity[(l + 1) * rows - STEPS : (l + 1) * rows, :]
        slot, at = divmod(l * STEPS, SUBLANES)
        a, b = ordered(odd, first, last)
        near[levels * STEPS + slot, at : at + STEPS, :] = a
        far[levels * STEPS + slot, at : at + STEPS, :] = b
    copies[1].wait()
    send_rows(grid, control, near, far)


def send_rows(grid, field, near, far):
    odd = is_odd("gy")
    for l in range(grid.levels):
        for r in range(STEPS):
            first = field[grid.members_at(l, r), :]
            last = field[grid.members_at(l, grid.rows - STEPS + r), :]
            near[l * STEPS + r], far[l * STEPS + r] = ordered(odd, first, last)


def field_columns(grid, field, got, near, far, edges):
    odd = is_odd("gy")
    for q in range(grid.packs):
        here = []
        for k in range(q * grid.per, min(grid.ring, (q + 1) * grid.per)):
            here.append(edges_of(grid, lambda l: grid.ring_row(field, got, odd, l, k)))
            edges[k] = here[-1]
        near[q], far[q] = ordered(is_odd("gx"), *packed(grid, here))


def columns_kernel(grid, control, diffusivity, got_near, got_far, near, far, edges, ring, ring_edges):
    got = (got_near, got_far)
    field_columns(grid, control, got, near, far, edges)
    odd = is_odd("gy")
    for l in range(grid.levels):
        slot, at = divmod(l * STEPS, SUBLANES)
        from_near, from_far = (g[grid.levels * STEPS + slot, at : at + STEPS, :] for g in got)
        after, before = ordered(odd, from_far, from_near)
        base = l * grid.ring
        ring[base : base + STEPS, :] = before
        ring[base + STEPS : base + STEPS + grid.rows, :] = diffusivity[l * grid.rows : (l + 1) * grid.rows, :]
        ring[base + STEPS + grid.rows : base + grid.ring, :] = after
    ring_edges[...] = edges_of(grid, lambda l: ring[l * grid.ring : (l + 1) * grid.ring, :], grid.ring)
    spaced = [ring_edges[pl.ds(i, grid.packs, stride=grid.per), :] for i in range(grid.per)]
    a, b = ordered(is_odd("gx"), *packed(grid, spaced, grid.packs))
    near[grid.packs, : grid.packs, :] = a
    far[grid.packs, : grid.packs, :] = b


def back_columns_kernel(grid, back, got_near, got_far, near, far, edges):
    field_columns(grid, back, (got_near, got_far), near, far, edges)


def main_steps(grid, steps, field, ring, got, keep, out):
    odd = is_odd("gy")
    keep[...] = 1.0 - 4.0 * ring[...]
    for l in range(grid.levels):
        rows = [grid.ring_row(field, got, odd, l, k) for k in range(grid.ring)]
        for y, row in enumerate(steps(rows, row_reader(ring, l * grid.ring), row_reader(keep, l * grid.ring))):
            out[l * grid.rows + y] = row


def spread_main_kernel(grid, control, ring, got_near, got_far, perturb_hbm, main, perturb, keep, sem):
    copy = pltpu.make_async_copy(perturb_hbm, perturb, sem)
    copy.start()
    main_steps(grid, spread_steps, control, ring, (got_near, got_far), keep, main)
    copy.wait()


def adjoint_main_kernel(grid, back, ring, got_near, got_far, main, keep):
    main_steps(grid, adjoint_steps, back, ring, (got_near, got_far), keep, main)


def sides(col_near, col_far, q):
    east, west = ordered(is_odd("gx"), col_far[q], col_near[q])
    return west, east


def strip_steps(grid, steps, edges, col_near, col_far, strip_ring, strip_keep, ends):
    strip_keep[...] = 1.0 - 4.0 * strip_ring[...]
    field = []
    for k in range(grid.ring):
        q, i = divmod(k, grid.per)
        field.append(strip_of(grid, edges[k], *sides(col_near, col_far, q), i))
    for y, strip in enumerate(steps(field, row_reader(strip_ring, 0), row_reader(strip_keep, 0))):
        ends[y] = joined(grid, strip)


def spread_kernel(grid, main, edges, ring_edges, col_near, col_far, perturb, partial, strip_ring, strip_keep, ends, spread):
    west, east = (side[: grid.packs] for side in sides(col_near, col_far, grid.packs))
    for i in range(grid.per):
        at = pl.ds(i, grid.packs, stride=grid.per)
        strip_ring[at, :] = strip_of(grid, ring_edges[at, :], west, east, i, grid.packs)
    strip_steps(grid, spread_steps, edges, col_near, col_far, strip_ring, strip_keep, ends)
    members, variables, levels, rows, _ = perturb.shape
    for l in range(levels):
        for y in range(rows):
            spread[grid.members_at(l, y), :] = merged(grid, main[l * rows + y], ends[y], l)
    tile = 2 * SUBLANES
    for l in range(levels):
        for start in range(0, rows, tile):
            here = [spread[(m * levels + l) * rows + start : (m * levels + l) * rows + start + tile, :] for m in range(members)]
            for v in range(variables):
                total = perturb[0, v, l, start : start + tile, :].astype(jnp.float32) * here[0]
                for m in range(1, members):
                    total = total + perturb[m, v, l, start : start + tile, :].astype(jnp.float32) * here[m]
                partial[v * levels + l, start : start + tile, :] = total


def back_kernel(grid, scale, increment, obs_count, obs_weight, perturb, back, near, far):
    members, variables, levels, rows, _ = perturb.shape
    tile = 2 * SUBLANES
    for l in range(levels):
        for start in range(0, rows, tile):
            at = slice(start, start + tile)
            seen = obs_count[l, at, :].astype(jnp.float32) * (scale * scale)
            weighted = [seen * obs_weight[v] * increment[v * levels + l, at, :] for v in range(variables)]
            for m in range(members):
                total = perturb[m, 0, l, at, :].astype(jnp.float32) * weighted[0]
                for v in range(1, variables):
                    total = total + perturb[m, v, l, at, :].astype(jnp.float32) * weighted[v]
                base = (m * levels + l) * rows
                back[base + start : base + start + tile, :] = total
    send_rows(grid, back, near, far)


def adjoint_kernel(grid, control, main, edges, strip_ring, col_near, col_far, out, strip_keep, ends):
    strip_steps(grid, adjoint_steps, edges, col_near, col_far, strip_ring, strip_keep, ends)
    for l in range(grid.levels):
        for y in range(grid.rows):
            at = grid.members_at(l, y)
            out[at, :] = control[at, :] + merged(grid, main[l * grid.rows + y], ends[y], l)


def shape_of(*shape):
    return jax.ShapeDtypeStruct(shape, jnp.float32)


def shards(control, perturb, obs_count, obs_weight, diffusivity):
    members, levels, rows, lanes = control.shape
    variables = perturb.shape[1]
    ways = lax.axis_size("mem")
    scale = 1.0 / math.sqrt(members * ways - 1)
    count = members * levels
    grid = Grid(members, levels, rows)
    assert members == SUBLANES and lanes == LANES and grid.block >= 8 * STEPS
    vmem = pl.BlockSpec(memory_space=pltpu.VMEM)
    hbm = pl.BlockSpec(memory_space=pltpu.HBM)
    f32 = jnp.float32

    def call(kernel, name, *args, work=0, **kwargs):
        cost = pl.CostEstimate(flops=work, bytes_accessed=work, transcendentals=0) if work else None
        return pl.pallas_call(lambda *refs: kernel(grid, *refs), name=name, compiler_params=PARAMS, cost_estimate=cost, **kwargs)(*args)

    def in_hbm(array):
        return pltpu.with_memory_space_constraint(array, pltpu.HBM)

    ring_shape, strip_shape = (levels * grid.ring, lanes), (grid.ring, lanes)
    edges_shape = shape_of(grid.ring, SUBLANES, lanes)
    main_shape = shape_of(levels * rows, SUBLANES, lanes)
    edge = shape_of(levels * STEPS + -(-levels * STEPS // SUBLANES), SUBLANES, lanes)
    near, far, flat, flat_diff = call(
        rows_kernel,
        "rows",
        in_hbm(control.reshape(count * rows, lanes)),
        in_hbm(diffusivity.reshape(levels * rows, lanes)),
        out_shape=(edge, edge, shape_of(count * rows, lanes), shape_of(levels * rows, lanes)),
        in_specs=[hbm, hbm],
        scratch_shapes=[pltpu.SemaphoreType.DMA((2,))],
    )
    got = swap(near, far, "gy")
    edge = shape_of(grid.packs + 1, SUBLANES, lanes)
    near, far, edges, ring, ring_edges = call(
        columns_kernel,
        "columns",
        flat,
        flat_diff,
        *got,
        out_shape=(edge, edge, edges_shape, shape_of(*ring_shape), shape_of(*strip_shape)),
    )
    sides = swap(near, far, "gx")
    main, held = call(
        spread_main_kernel,
        "spread_main",
        flat,
        ring,
        *got,
        in_hbm(perturb),
        work=6 << 20,
        out_shape=(main_shape, jax.ShapeDtypeStruct(perturb.shape, perturb.dtype)),
        in_specs=[vmem] * 4 + [hbm],
        scratch_shapes=[pltpu.VMEM(ring_shape, f32), pltpu.SemaphoreType.DMA],
    )
    partial, strip_ring = call(
        spread_kernel,
        "spread",
        main,
        edges,
        ring_edges,
        *sides,
        held,
        out_shape=(shape_of(variables * levels, rows, lanes), shape_of(*strip_shape)),
        scratch_shapes=[
            pltpu.VMEM(strip_shape, f32),
            pltpu.VMEM((rows, SUBLANES, lanes), f32),
            pltpu.VMEM((count * rows, lanes), f32),
        ],
    )

    parts = lax.all_to_all(partial.reshape(ways, -1, lanes), "mem", 0, 0)
    mine = jnp.sum(parts, axis=0)
    increment = lax.all_to_all(jnp.broadcast_to(mine, parts.shape), "mem", 0, 0)
    increment = increment.reshape(variables * levels, rows, lanes)

    edge = shape_of(levels * STEPS, SUBLANES, lanes)
    back, near, far = call(
        lambda grid, *refs: back_kernel(grid, scale, *refs),
        "back",
        increment,
        obs_count,
        obs_weight,
        held,
        out_shape=(shape_of(count * rows, lanes), edge, edge),
        in_specs=[vmem, vmem, pl.BlockSpec(memory_space=pltpu.SMEM), vmem],
    )
    got = swap(near, far, "gy")
    edge = shape_of(grid.packs, SUBLANES, lanes)
    near, far, edges = call(back_columns_kernel, "back_columns", back, *got, out_shape=(edge, edge, edges_shape))
    sides = swap(near, far, "gx")
    main = call(
        adjoint_main_kernel,
        "adjoint_main",
        back,
        ring,
        *got,
        work=6 << 20,
        out_shape=main_shape,
        scratch_shapes=[pltpu.VMEM(ring_shape, f32)],
    )
    out = call(
        adjoint_kernel,
        "adjoint",
        flat,
        main,
        edges,
        strip_ring,
        *sides,
        out_shape=shape_of(count * rows, lanes),
        scratch_shapes=[pltpu.VMEM(strip_shape, f32), pltpu.VMEM((rows, SUBLANES, lanes), f32)],
    )
    return out.reshape(control.shape)


def solution(mesh):
    placed = (
        P("mem", None, "gy", "gx"),
        P("mem", None, None, "gy", "gx"),
        P(None, "gy", "gx"),
        P(),
        P(None, "gy", "gx"),
    )
    return jax.shard_map(
        shards, mesh=mesh, in_specs=placed, out_specs=P("mem", None, "gy", "gx"), check_vma=False
    )
```

time: 505 us -> 76.5 us (0.15)
  the two profiles are of different devices: /device:TPU:486 before, /device:TPU:24 now
where the time goes in v3:
time: 76.5 us; the launch traced here: 75.4 us
  starting transfers between devices  36.4 us (48%)
  blocking collectives  22.3 us (29%)
  Pallas kernels  8.92 us (12%)
  waiting for transfers between devices  7.62 us (10%)
    ppermute x8, starting transfers between devices, swap(): out.append(lax.ppermute(value, axis, pairs))  36.4 us
    all_to_all x1, blocking collectives, shards(): parts = lax.all_to_all(partial.reshape(ways, -1, lanes), 'mem', 0, 0)  12.1 us
    all_to_all x1, blocking collectives, shards(): increment = lax.all_to_all(jnp.broadcast_to(mine, parts.shape), 'mem', 0, 0)  10.2 us
    pallas_call x8, Pallas kernels, call(): pl.pallas_call(lambda *refs: kernel(grid, *refs), name=name, compiler_par...  8.92 us
    ppermute x8, waiting for transfers between devices, swap(): out.append(lax.ppermute(value, axis, pairs))  7.62 us
  transfers between devices with their start and end apart: 8, of which 2 were waited for; matrix products, arithmetic and copies ran while one was open for 0% of the time, Pallas kernels for 4%

profile of v3, /device:TPU:24, one launch (start us, length us, event | category | flops | bytes accessed | tf_op | source)
XLA Modules:
  0.0 75.4 jit_solution(16852340357375195557)
XLA Ops:
  0.0 1.1 %rows.1 = (f32[14,8,128]{2,1,0:T(8,128)S(1)}, f32[14,8,128]{2,1,0:T(8,128)S(1)}, f32[768,128]{1,0:T(8,128)S(1)}, f32[96,128]{1,0:T(8,128)S(1)}) custom-call(f32[768,128]{1,0:T(8,128)} %bitcast.7, f32[96,128]{1,0:T(8,128)} %bitcast.8), custom_call_target="tpu_custom_call" | custom-call | tf_op jit(solution)/shard_map/rows/pallas_call | solution.py:298
  1.1 2.7 %collective-permute-start = (f32[14,8,128]{2,1,0:T(8,128)S(1)}, f32[14,8,128]{2,1,0:T(8,128)S(1)}, u32[]{:S(2)}, u32[]{:S(2)}) collective-permute-start(f32[14,8,128]{2,1,0:T(8,128)S(1)} %get-tuple-element.26), channel_id=1, source_target_pairs={{0,1},{1,0},{2,3},{3,2},{4,5},{5,4},{6,7},{7,6},{8,9},{9,8},{10,11... | collective-permute-start | bytes 172040 | tf_op jit(solution)/shard_map/ppermute | solution.py:23
  3.8 4.3 %collective-permute-start.1 = (f32[14,8,128]{2,1,0:T(8,128)S(1)}, f32[14,8,128]{2,1,0:T(8,128)S(1)}, u32[]{:S(2)}, u32[]{:S(2)}) collective-permute-start(f32[14,8,128]{2,1,0:T(8,128)S(1)} %get-tuple-element.27), channel_id=1, source_target_pairs={{1,2},{2,1},{3,4},{4,3},{5,6},{6,5},{7,8},{8,7},{9,10},{10,9},{11,... | collective-permute-start | bytes 172040 | tf_op jit(solution)/shard_map/ppermute | solution.py:23
  8.1 0.0 collective-permute-done.refs_2_
  8.1 3.8 %collective-permute-done.1.refs_3_ = f32[14,8,128]{2,1,0:T(8,128)S(1)} collective-permute-done((f32[14,8,128]{2,1,0:T(8,128)S(1)}, f32[14,8,128]{2,1,0:T(8,128)S(1)}, u32[]{:S(2)}, u32[]{:S(2)}) %collective-permute-start.1) | collective-permute-done | bytes 57376 | tf_op jit(solution)/shard_map/ppermute | solution.py:23
  11.9 0.5 columns.1
  12.4 9.1 %collective-permute-start.2 = (f32[5,8,128]{2,1,0:T(8,128)S(1)}, f32[5,8,128]{2,1,0:T(8,128)S(1)}, u32[]{:S(2)}, u32[]{:S(2)}) collective-permute-start(f32[5,8,128]{2,1,0:T(8,128)S(1)} %get-tuple-element.32), channel_id=1, source_target_pairs={{0,16},{16,0},{32,48},{48,32},{1,17},{17,1},{33,49},{49,33},{2,18}... | collective-permute-start | bytes 61448 | tf_op jit(solution)/shard_map/ppermute | solution.py:23
  21.5 0.7 collective-permute-start.3
  22.2 2.2 %spread_main.1 = (f32[96,8,128]{2,1,0:T(8,128)S(1)}, bf16[8,6,3,32,128]{4,3,2,1,0:T(8,128)(2,1)S(1)}) custom-call(f32[768,128]{1,0:T(8,128)S(1)} %get-tuple-element.24.refs_0_, f32[120,128]{1,0:T(8,128)S(1)} %get-tuple-element.28.refs_1_, f32[14,8,128]{2,1,0:T(8,128)S(1)} %collective-permute-done.refs_2_, f32[14,8,128]{2,1,0:T(8,128)S(1)} %collective-permute-done.1.refs_3_, ...), custom_call_target="tpu_custom_call" | custom-call | flops 6291456 | bytes 6291456 | tf_op jit(solution)/shard_map/spread_main/pallas_call | solution.py:298
  24.4 0.0 collective-permute-done.2.refs_3_
  24.4 0.0 collective-permute-done.3.refs_4_
  24.5 1.1 %spread.1 = (f32[18,32,128]{2,1,0:T(8,128)S(1)}, f32[40,128]{1,0:T(8,128)S(1)}) custom-call(f32[96,8,128]{2,1,0:T(8,128)S(1)} %get-tuple-element.29.refs_0_, f32[40,8,128]{2,1,0:T(8,128)S(1)} %get-tuple-element.30.refs_1_, f32[40,128]{1,0:T(8,128)S(1)} %get-tuple-element.31.refs_2_, f32[5,8,128]{2,1,0:T(8,128)S(1)} %collective-permute-done.2.refs_3_, ...), custom_call_target="tpu_custom_call" | custom-call | tf_op jit(solution)/shard_map/spread/pallas_call | solution.py:298
  25.6 0.0 copy-start
  25.6 0.0 copy-start.1
  25.6 12.1 %all_to_all.10 = f32[8,72,128]{2,1,0:T(8,128)S(1)} all-to-all(f32[8,72,128]{2,1,0:T(8,128)S(1)} %bitcast.6), channel_id=1, replica_groups=mesh['mem'=8,'gx'=4,'gy'=16] {'mem'}, dimensions={0} | all-to-all | bytes 589824 | tf_op jit(solution)/shard_map/all_to_all | solution.py:355
  37.7 10.2 %all_to_all.11 = f32[8,72,128]{2,1,0:T(8,128)S(1)} all-to-all(f32[8,72,128]{2,1,0:T(8,128)S(1)} %broadcast_in_dim.3), channel_id=1, replica_groups=mesh['mem'=8,'gx'=4,'gy'=16] {'mem'}, dimensions={0} | all-to-all | bytes 589824 | tf_op jit(solution)/shard_map/all_to_all | solution.py:357
  48.0 0.0 copy-done
  48.0 0.0 copy-done.1
  48.0 0.8 %back.1 = (f32[768,128]{1,0:T(8,128)S(1)}, f32[12,8,128]{2,1,0:T(8,128)S(1)}, f32[12,8,128]{2,1,0:T(8,128)S(1)}) custom-call(f32[18,32,128]{2,1,0:T(8,128)S(1)} %bitcast.5, s32[3,32,128]{2,1,0:T(8,128)S(1)} %copy-done, f32[6]{0:T(128)S(1)} %copy-done.1, bf16[8,6,3,32,128]{4,3,2,1,0:T(8,128)(2,1)S(1)} %get-tuple-element.34.refs_5_.refs_3_), custom_call_target="tpu_custom_call" | custom-call | tf_op jit(solution)/shard_map/back/pallas_call | solution.py:298
  48.8 1.9 %collective-permute-start.4 = (f32[12,8,128]{2,1,0:T(8,128)S(1)}, f32[12,8,128]{2,1,0:T(8,128)S(1)}, u32[]{:S(2)}, u32[]{:S(2)}) collective-permute-start(f32[12,8,128]{2,1,0:T(8,128)S(1)} %get-tuple-element.37), channel_id=1, source_target_pairs={{0,1},{1,0},{2,3},{3,2},{4,5},{5,4},{6,7},{7,6},{8,9},{9,8},{10,11... | collective-permute-start | bytes 147464 | tf_op jit(solution)/shard_map/ppermute | solution.py:23
  50.7 4.3 %collective-permute-start.5 = (f32[12,8,128]{2,1,0:T(8,128)S(1)}, f32[12,8,128]{2,1,0:T(8,128)S(1)}, u32[]{:S(2)}, u32[]{:S(2)}) collective-permute-start(f32[12,8,128]{2,1,0:T(8,128)S(1)} %get-tuple-element.38), channel_id=1, source_target_pairs={{1,2},{2,1},{3,4},{4,3},{5,6},{6,5},{7,8},{8,7},{9,10},{10,9},{11,... | collective-permute-start | bytes 147464 | tf_op jit(solution)/shard_map/ppermute | solution.py:23
  55.1 0.0 collective-permute-done.4.refs_2_.refs_1_
  55.1 3.8 %collective-permute-done.5.refs_3_.refs_2_ = f32[12,8,128]{2,1,0:T(8,128)S(1)} collective-permute-done((f32[12,8,128]{2,1,0:T(8,128)S(1)}, f32[12,8,128]{2,1,0:T(8,128)S(1)}, u32[]{:S(2)}, u32[]{:S(2)}) %collective-permute-start.5) | collective-permute-done | bytes 49184 | tf_op jit(solution)/shard_map/ppermute | solution.py:23
  58.8 0.4 back_columns.1
  59.2 12.7 %collective-permute-start.6 = (f32[4,8,128]{2,1,0:T(8,128)S(1)}, f32[4,8,128]{2,1,0:T(8,128)S(1)}, u32[]{:S(2)}, u32[]{:S(2)}) collective-permute-start(f32[4,8,128]{2,1,0:T(8,128)S(1)} %get-tuple-element.41), channel_id=1, source_target_pairs={{0,16},{16,0},{32,48},{48,32},{1,17},{17,1},{33,49},{49,33},{2,18}... | collective-permute-start | bytes 49160 | tf_op jit(solution)/shard_map/ppermute | solution.py:23
  72.0 0.7 collective-permute-start.7
  72.6 1.0 %adjoint_main.1.refs_1_ = f32[96,8,128]{2,1,0:T(8,128)S(1)} custom-call(f32[768,128]{1,0:T(8,128)S(1)} %get-tuple-element.36.refs_0_, f32[120,128]{1,0:T(8,128)S(1)} %get-tuple-element.28.refs_1_, f32[12,8,128]{2,1,0:T(8,128)S(1)} %collective-permute-done.4.refs_2_.refs_1_, f32[12,8,128]{2,1,0:T(8,128)S(1)} %collective-permute-done.5.refs_3_.refs_2_), custom_call_target="tpu_custom_call" | custom-call | flops 6291456 | bytes 6291456 | tf_op jit(solution)/shard_map/adjoint_main/pallas_call | solution.py:298
  73.7 0.0 collective-permute-done.6.refs_4_
  73.7 0.0 collective-permute-done.7.refs_5_
  73.7 1.8 %adjoint.1 = f32[768,128]{1,0:T(8,128)} custom-call(f32[768,128]{1,0:T(8,128)S(1)} %get-tuple-element.24.refs_0_, f32[96,8,128]{2,1,0:T(8,128)S(1)} %adjoint_main.1.refs_1_, f32[40,8,128]{2,1,0:T(8,128)S(1)} %get-tuple-element.39.refs_2_, f32[40,128]{1,0:T(8,128)S(1)} %get-tuple-element.40.refs_3_, f32[4,8,128]{2,1,0:T(8,128)S(1)} %collective-permute-done.6.refs_4_, ...), custom_call_target="tpu_custom_call" | custom-call | tf_op jit(solution)/shard_map/adjoint/pallas_call | solution.py:298
  (2 shorter events, 0.0 us)
Async XLA Ops:
  1.1 7.0 %collective-permute-start = (f32[14,8,128]{2,1,0:T(8,128)S(1)}, f32[14,8,128]{2,1,0:T(8,128)S(1)}, u32[]{:S(2)}, u32[]{:S(2)}) collective-permute-start(f32[14,8,128]{2,1,0:T(8,128)S(1)} %get-tuple-element.26), channel_id=1, source_target_pairs={{0,1},{1,0},{2,3},{3,2},{4,5},{5,4},{6,7},{7,6},{8,9},{9,8},{10,11... | collective-permute-start | bytes 172040 | tf_op jit(solution)/shard_map/ppermute | solution.py:23
  3.8 8.2 %collective-permute-start.1 = (f32[14,8,128]{2,1,0:T(8,128)S(1)}, f32[14,8,128]{2,1,0:T(8,128)S(1)}, u32[]{:S(2)}, u32[]{:S(2)}) collective-permute-start(f32[14,8,128]{2,1,0:T(8,128)S(1)} %get-tuple-element.27), channel_id=1, source_target_pairs={{1,2},{2,1},{3,4},{4,3},{5,6},{6,5},{7,8},{8,7},{9,10},{10,9},{11,... | collective-permute-start | bytes 172040 | tf_op jit(solution)/shard_map/ppermute | solution.py:23
  12.4 12.0 %collective-permute-start.2 = (f32[5,8,128]{2,1,0:T(8,128)S(1)}, f32[5,8,128]{2,1,0:T(8,128)S(1)}, u32[]{:S(2)}, u32[]{:S(2)}) collective-permute-start(f32[5,8,128]{2,1,0:T(8,128)S(1)} %get-tuple-element.32), channel_id=1, source_target_pairs={{0,16},{16,0},{32,48},{48,32},{1,17},{17,1},{33,49},{49,33},{2,18}... | collective-permute-start | bytes 61448 | tf_op jit(solution)/shard_map/ppermute | solution.py:23
  21.5 2.9 %collective-permute-start.3 = (f32[5,8,128]{2,1,0:T(8,128)S(1)}, f32[5,8,128]{2,1,0:T(8,128)S(1)}, u32[]{:S(2)}, u32[]{:S(2)}) collective-permute-start(f32[5,8,128]{2,1,0:T(8,128)S(1)} %get-tuple-element.33), channel_id=1, source_target_pairs={{16,32},{32,16},{17,33},{33,17},{18,34},{34,18},{19,35},{35,19},{2... | collective-permute-start | bytes 61448 | tf_op jit(solution)/shard_map/ppermute | solution.py:23
  25.6 22.4 %copy-start = (s32[3,32,128]{2,1,0:T(8,128)S(1)}, s32[3,32,128]{2,1,0:T(8,128)}, u32[]{:S(2)}) copy-start(s32[3,32,128]{2,1,0:T(8,128)} %refs_1_.1) | copy-start | bytes 147460
  25.6 22.4 %copy-start.1 = (f32[6]{0:T(128)S(1)}, f32[6]{0:T(128)}, u32[]{:S(2)}) copy-start(f32[6]{0:T(128)} %refs_2_.1) | copy-start | bytes 76
  48.8 6.3 %collective-permute-start.4 = (f32[12,8,128]{2,1,0:T(8,128)S(1)}, f32[12,8,128]{2,1,0:T(8,128)S(1)}, u32[]{:S(2)}, u32[]{:S(2)}) collective-permute-start(f32[12,8,128]{2,1,0:T(8,128)S(1)} %get-tuple-element.37), channel_id=1, source_target_pairs={{0,1},{1,0},{2,3},{3,2},{4,5},{5,4},{6,7},{7,6},{8,9},{9,8},{10,11... | collective-permute-start | bytes 147464 | tf_op jit(solution)/shard_map/ppermute | solution.py:23
  50.7 8.1 %collective-permute-start.5 = (f32[12,8,128]{2,1,0:T(8,128)S(1)}, f32[12,8,128]{2,1,0:T(8,128)S(1)}, u32[]{:S(2)}, u32[]{:S(2)}) collective-permute-start(f32[12,8,128]{2,1,0:T(8,128)S(1)} %get-tuple-element.38), channel_id=1, source_target_pairs={{1,2},{2,1},{3,4},{4,3},{5,6},{6,5},{7,8},{8,7},{9,10},{10,9},{11,... | collective-permute-start | bytes 147464 | tf_op jit(solution)/shard_map/ppermute | solution.py:23
  59.2 14.4 %collective-permute-start.6 = (f32[4,8,128]{2,1,0:T(8,128)S(1)}, f32[4,8,128]{2,1,0:T(8,128)S(1)}, u32[]{:S(2)}, u32[]{:S(2)}) collective-permute-start(f32[4,8,128]{2,1,0:T(8,128)S(1)} %get-tuple-element.41), channel_id=1, source_target_pairs={{0,16},{16,0},{32,48},{48,32},{1,17},{17,1},{33,49},{49,33},{2,18}... | collective-permute-start | bytes 49160 | tf_op jit(solution)/shard_map/ppermute | solution.py:23
  72.0 1.7 %collective-permute-start.7 = (f32[4,8,128]{2,1,0:T(8,128)S(1)}, f32[4,8,128]{2,1,0:T(8,128)S(1)}, u32[]{:S(2)}, u32[]{:S(2)}) collective-permute-start(f32[4,8,128]{2,1,0:T(8,128)S(1)} %get-tuple-element.42), channel_id=1, source_target_pairs={{16,32},{32,16},{17,33},{33,17},{18,34},{34,18},{19,35},{35,19},{2... | collective-permute-start | bytes 49160 | tf_op jit(solution)/shard_map/ppermute | solution.py:23

commit v4 on v3

v4 whole, which is shorter than its diff:
```python
import math

import jax
import jax.numpy as jnp
from jax import lax
from jax.experimental import pallas as pl
from jax.experimental.pallas import tpu as pltpu
from jax.sharding import PartitionSpec as P


STEPS = 4
LANES = 128
SUBLANES = 8
PARAMS = pltpu.CompilerParams(vmem_limit_bytes=16 << 20)


def swap(near, far, axis):
    size = lax.axis_size(axis)
    out = []
    for value, start in ((near, 0), (far, 1)):
        pairs = []
        for i in range(start, size - 1, 2):
            pairs += [(i, i + 1), (i + 1, i)]
        out.append(lax.ppermute(value, axis, pairs))
    return out


def is_odd(axis):
    return lax.rem(lax.axis_index(axis), 2) == 1


def ordered(odd, first, last):
    return jnp.where(odd, first, last), jnp.where(odd, last, first)


class Grid:
    def __init__(self, members, levels, rows):
        self.members, self.levels, self.rows = members, levels, rows
        self.wide = rows + 4 * STEPS
        self.ring = rows + 2 * STEPS
        self.block = LANES // levels // STEPS * STEPS
        self.per = self.block // STEPS
        self.wide_packs = -(-self.wide // self.per)
        self.packs = -(-self.ring // self.per)
        self.padded = -(-self.wide_packs * self.per // SUBLANES) * SUBLANES

    def members_at(self, level, y):
        return pl.ds(level * self.rows + y, self.members, stride=self.levels * self.rows)

    def rim_at(self, level, r):
        return pl.ds(level * self.members * STEPS + r, self.members, stride=STEPS)

    def wide_row(self, field, got, odd, level, k):
        y = k - 2 * STEPS
        if 0 <= y < self.rows:
            return field[self.members_at(level, y), :]
        before = y < 0
        at = level * 2 * STEPS + (k if before else y - self.rows)
        near, far = got
        after_value, before_value = ordered(odd, far[at], near[at])
        return before_value if before else after_value

    def ring_row(self, field, before, after, level, k):
        y = k - STEPS
        if y < 0:
            return before[self.rim_at(level, k), :]
        if y >= self.rows:
            return after[self.rim_at(level, y - self.rows), :]
        return field[self.members_at(level, y), :]

    def tile_of(self, ref, plane, j):
        t = plane * (self.ring // SUBLANES) + j
        return t // (ref.shape[1] // SUBLANES), pl.ds(t % (ref.shape[1] // SUBLANES) * SUBLANES, SUBLANES)

    def lanes(self, rows=SUBLANES):
        lane = lax.broadcasted_iota(jnp.int32, (rows, LANES), 1)
        return lax.rem(lane, self.block)


def within(place, start, size):
    return (place >= start) & (place < start + size)


def rolled(value, shift):
    shift %= LANES
    return pltpu.roll(value, shift, 1) if shift else value


def edges_of(grid, value_of, rows=SUBLANES):
    lane = lax.broadcasted_iota(jnp.int32, (rows, LANES), 1)
    out = jnp.zeros((rows, LANES), jnp.float32)
    for l in range(grid.levels):
        base = l * grid.block
        out = jnp.where(within(lane, base, 4 * STEPS), rolled(value_of(l), base + 2 * STEPS), out)
    return out


def packed(grid, edges, rows=SUBLANES):
    place = grid.lanes(rows)
    first = jnp.zeros((rows, LANES), jnp.float32)
    last = first
    for i, value in enumerate(edges):
        mask = within(place, i * STEPS, STEPS)
        first = jnp.where(mask, rolled(value, (i - 2) * STEPS), first)
        last = jnp.where(mask, rolled(value, (i - 1) * STEPS), last)
    return first, last


def strip_of(grid, edges, west, east, i, rows=SUBLANES):
    place = grid.lanes(rows)
    out = jnp.where(place < 2 * STEPS, edges, 0.0)
    out = jnp.where(within(place, 6 * STEPS, 2 * STEPS), rolled(edges, 4 * STEPS), out)
    out = jnp.where(within(place, 2 * STEPS, STEPS), rolled(east, (2 - i) * STEPS), out)
    return jnp.where(within(place, 5 * STEPS, STEPS), rolled(west, (5 - i) * STEPS), out)


def joined(grid, strip):
    return jnp.where(grid.lanes() < 2 * STEPS, strip, rolled(strip, -4 * STEPS))


def merged(grid, main, ends, level):
    lane = lax.broadcasted_iota(jnp.int32, (SUBLANES, LANES), 1)
    outer = (lane < STEPS) | (lane >= LANES - STEPS)
    return jnp.where(outer, rolled(ends, LANES - 2 * STEPS - level * grid.block), main)


def lateral(value):
    return pltpu.roll(value, 1, 1) + pltpu.roll(value, LANES - 1, 1)


def spread_steps(field, coef, keep):
    for s in range(1, STEPS + 1):
        new = list(field)
        for k in range(s, len(field) - s):
            around = (field[k - 1] + field[k + 1]) + lateral(field[k])
            new[k] = keep(k) * field[k] + coef(k) * around
        field = new
    return field[STEPS:-STEPS]


def adjoint_steps(field, coef, keep):
    for s in range(1, STEPS + 1):
        flux = {k: coef(k) * field[k] for k in range(s - 1, len(field) - s + 1)}
        new = list(field)
        for k in range(s, len(field) - s):
            new[k] = keep(k) * field[k] + ((flux[k - 1] + flux[k + 1]) + lateral(flux[k]))
        field = new
    return field[STEPS:-STEPS]


def row_reader(ref, start):
    return lambda k: jnp.broadcast_to(ref[pl.ds(start + k, 1), :], (SUBLANES, LANES))


def rows_kernel(grid, control_hbm, diffusivity_hbm, count_hbm, near, far, control, diffusivity, seen, count, sems):
    levels, rows = grid.levels, grid.rows
    depth = 2 * STEPS
    copies = [
        pltpu.make_async_copy(diffusivity_hbm, diffusivity, sems.at[0]),
        pltpu.make_async_copy(count_hbm, count, sems.at[1]),
        pltpu.make_async_copy(control_hbm, control, sems.at[2]),
    ]
    for copy in copies:
        copy.start()
    odd = is_odd("gy")
    copies[0].wait()
    copies[1].wait()
    seen[...] = count[...].astype(jnp.float32)
    at = levels * depth
    for l in range(levels):
        first = diffusivity[l * rows : l * rows + depth, :]
        last = diffusivity[(l + 1) * rows - depth : (l + 1) * rows, :]
        near[at + l], far[at + l] = ordered(odd, first, last)
        first = seen[l * rows : l * rows + STEPS, :]
        last = seen[(l + 1) * rows - STEPS : (l + 1) * rows, :]
        slot, sub = divmod(l * STEPS, SUBLANES)
        a, b = ordered(odd, first, last)
        near[at + levels + slot, sub : sub + STEPS, :] = a
        far[at + levels + slot, sub : sub + STEPS, :] = b
    copies[2].wait()
    for l in range(levels):
        for r in range(depth):
            first = control[grid.members_at(l, r), :]
            last = control[grid.members_at(l, rows - depth + r), :]
            near[l * depth + r], far[l * depth + r] = ordered(odd, first, last)


def turned(value):
    return pltpu.roll(value, STEPS, 0)


def upper():
    return lax.broadcasted_iota(jnp.int32, (SUBLANES, LANES), 0) < STEPS


def perturb_rows_kernel(grid, order, perturb_hbm, near, far, perturb, sems):
    members, variables, levels, rows, _ = perturb.shape
    copies = [
        pltpu.make_async_copy(perturb_hbm.at[pl.ds(2 * q, 2)], perturb.at[pl.ds(2 * q, 2)], sems.at[q]) for q in range(members // 2)
    ]
    for copy in copies:
        copy.start()
    odd = is_odd("gy")
    tile = 2 * SUBLANES
    for q, copy in enumerate(copies):
        copy.wait()
        for v in range(variables):
            for l in range(levels):
                heads = [perturb[2 * q + j, v, l, :tile, :].astype(jnp.float32)[:SUBLANES] for j in range(2)]
                tails = [perturb[2 * q + j, v, l, rows - tile :, :].astype(jnp.float32)[SUBLANES:] for j in range(2)]
                first = jnp.where(upper(), heads[0], turned(heads[1]))
                last = jnp.where(upper(), turned(tails[0]), tails[1])
                at = (v * levels + l) * (members // 2) + q
                near[at], far[at] = ordered(odd, first, last)


def field_columns(grid, row_of, length, near, far, edges):
    for start in range(0, length, grid.per):
        here = []
        for k in range(start, min(length, start + grid.per)):
            here.append(edges_of(grid, lambda l: row_of(l, k)))
            edges[k] = here[-1]
        q = start // grid.per
        near[q], far[q] = ordered(is_odd("gx"), *packed(grid, here))


def columns_kernel(grid, control, diffusivity, got_near, got_far, near, far, edges, ring, ring_edges):
    got = (got_near, got_far)
    odd = is_odd("gy")
    field_columns(grid, lambda l, k: grid.wide_row(control, got, odd, l, k), grid.wide, near, far, edges)
    depth = 2 * STEPS
    for l in range(grid.levels):
        after, before = ordered(odd, got_far[grid.levels * depth + l], got_near[grid.levels * depth + l])
        base = l * grid.wide
        ring[base : base + depth, :] = before
        ring[base + depth : base + depth + grid.rows, :] = diffusivity[l * grid.rows : (l + 1) * grid.rows, :]
        ring[base + depth + grid.rows : base + grid.wide, :] = after
    ring_edges[...] = jnp.zeros(ring_edges.shape, jnp.float32)
    ring_edges[: grid.wide, :] = edges_of(grid, lambda l: ring[l * grid.wide : (l + 1) * grid.wide, :], grid.wide)
    packs = grid.wide_packs
    spaced = [ring_edges[pl.ds(i, packs, stride=grid.per), :] for i in range(grid.per)]
    a, b = ordered(is_odd("gx"), *packed(grid, spaced, packs))
    near[packs, :packs, :] = a
    far[packs, :packs, :] = b


def spread_main_kernel(grid, control, ring, got_near, got_far, main, keep):
    odd = is_odd("gy")
    keep[...] = 1.0 - 4.0 * ring[...]
    for l in range(grid.levels):
        rows = [grid.wide_row(control, (got_near, got_far), odd, l, k) for k in range(grid.wide)]
        at = l * grid.wide
        for y, row in enumerate(spread_steps(rows, row_reader(ring, at), row_reader(keep, at))):
            main[l * grid.ring + y] = row


def adjoint_main_kernel(grid, back, before, after, ring, main, keep):
    keep[...] = 1.0 - 4.0 * ring[...]
    for l in range(grid.levels):
        rows = [grid.ring_row(back, before, after, l, k) for k in range(grid.ring)]
        at = l * grid.wide + STEPS
        for y, row in enumerate(adjoint_steps(rows, row_reader(ring, at), row_reader(keep, at))):
            main[l * grid.rows + y] = row


def sides(col_near, col_far, q):
    east, west = ordered(is_odd("gx"), col_far[q], col_near[q])
    return west, east


def strip_steps(grid, steps, edges, length, skip, col_near, col_far, strip_ring, strip_keep, ends):
    strip_keep[...] = 1.0 - 4.0 * strip_ring[...]
    field = []
    for k in range(length):
        q, i = divmod(k, grid.per)
        field.append(strip_of(grid, edges[k], *sides(col_near, col_far, q), i))
    for y, strip in enumerate(steps(field, row_reader(strip_ring, skip), row_reader(strip_keep, skip))):
        ends[y] = joined(grid, strip)


def spread_kernel(
    grid,
    main,
    edges,
    ring_edges,
    col_near,
    col_far,
    perturb,
    rim_near,
    rim_far,
    partial,
    strip_ring,
    strip_keep,
    ends,
    spread,
    spread_before,
    spread_after,
):
    packs = grid.wide_packs
    west, east = (side[:packs] for side in sides(col_near, col_far, packs))
    strip_ring[...] = jnp.zeros(strip_ring.shape, jnp.float32)
    for i in range(grid.per):
        at = pl.ds(i, packs, stride=grid.per)
        strip_ring[at, :] = strip_of(grid, ring_edges[at, :], west, east, i, packs)
    strip_steps(grid, spread_steps, edges, grid.wide, 0, col_near, col_far, strip_ring, strip_keep, ends)
    members, variables, levels, rows, _ = perturb.shape
    for l in range(levels):
        for j in range(grid.ring):
            value = merged(grid, main[l * grid.ring + j], ends[j], l)
            y = j - STEPS
            if y < 0:
                spread_before[grid.rim_at(l, j), :] = value
            elif y >= rows:
                spread_after[grid.rim_at(l, y - rows), :] = value
            else:
                spread[grid.members_at(l, y), :] = value
    tile = 2 * SUBLANES
    odd = is_odd("gy")
    pairs = members // 2
    for l in range(levels):
        for start in range(0, rows, tile):
            here = [spread[(m * levels + l) * rows + start : (m * levels + l) * rows + start + tile, :] for m in range(members)]
            for v in range(variables):
                total = perturb[0, v, l, start : start + tile, :].astype(jnp.float32) * here[0]
                for m in range(1, members):
                    total = total + perturb[m, v, l, start : start + tile, :].astype(jnp.float32) * here[m]
                for j in range(2):
                    partial[grid.tile_of(partial, v * levels + l, start // SUBLANES + j)] = total[j * SUBLANES : (j + 1) * SUBLANES]
        rims = [(after, before) for after, before in zip(
            [spread_after[(l * pairs + q) * SUBLANES : (l * pairs + q + 1) * SUBLANES, :] for q in range(pairs)],
            [spread_before[(l * pairs + q) * SUBLANES : (l * pairs + q + 1) * SUBLANES, :] for q in range(pairs)],
        )]
        for v in range(variables):
            totals = [0.0, 0.0]
            for q in range(pairs):
                at = (v * levels + l) * pairs + q
                outer = ordered(odd, rim_far[at], rim_near[at])
                totals = [t + p * r for t, p, r in zip(totals, outer, rims[q])]
            after, before = (t + turned(t) for t in totals)
            partial[grid.tile_of(partial, v * levels + l, rows // SUBLANES)] = jnp.where(upper(), after, before)
    used = variables * levels * (grid.ring // SUBLANES)
    for t in range(used, partial.shape[0] * partial.shape[1] // SUBLANES):
        partial[grid.tile_of(partial, 0, t)] = jnp.zeros((SUBLANES, LANES), jnp.float32)


def back_kernel(
    grid,
    scale,
    increment,
    seen,
    obs_weight,
    perturb,
    rim_near,
    rim_far,
    got_near,
    got_far,
    back,
    back_before,
    back_after,
    edges,
    near,
    far,
):
    members, variables, levels, rows, _ = perturb.shape
    tile = 2 * SUBLANES
    odd = is_odd("gy")
    pairs = members // 2
    for l in range(levels):
        for start in range(0, rows, tile):
            factor = seen[l * rows + start : l * rows + start + tile, :] * (scale * scale)
            weighted = []
            for v in range(variables):
                at = [grid.tile_of(increment, v * levels + l, start // SUBLANES + j) for j in range(2)]
                weighted.append(factor * obs_weight[v] * jnp.concatenate([increment[at[0]], increment[at[1]]], axis=0))
            for m in range(members):
                total = perturb[m, 0, l, start : start + tile, :].astype(jnp.float32) * weighted[0]
                for v in range(1, variables):
                    total = total + perturb[m, v, l, start : start + tile, :].astype(jnp.float32) * weighted[v]
                base = (m * levels + l) * rows
                back[base + start : base + start + tile, :] = total
        slot, sub = divmod(l * STEPS, SUBLANES)
        slot += levels * 2 * STEPS + levels
        counts = ordered(odd, got_far[slot, sub : sub + STEPS, :], got_near[slot, sub : sub + STEPS, :])
        counts = [jnp.concatenate([c, c], axis=0) * (scale * scale) for c in counts]
        totals = [[0.0] * pairs, [0.0] * pairs]
        for v in range(variables):
            both = increment[grid.tile_of(increment, v * levels + l, rows // SUBLANES)]
            after = jnp.where(upper(), both, turned(both))
            before = jnp.where(upper(), turned(both), both)
            weighted = [c * obs_weight[v] * w for c, w in zip(counts, (after, before))]
            for q in range(pairs):
                at = (v * levels + l) * pairs + q
                for side, p in enumerate(ordered(odd, rim_far[at], rim_near[at])):
                    totals[side][q] = totals[side][q] + p * weighted[side]
        for q in range(pairs):
            at = slice((l * pairs + q) * SUBLANES, (l * pairs + q + 1) * SUBLANES)
            back_after[at, :] = totals[0][q]
            back_before[at, :] = totals[1][q]
    field_columns(grid, lambda l, k: grid.ring_row(back, back_before, back_after, l, k), grid.ring, near, far, edges)


def adjoint_kernel(grid, control, main, edges, strip_ring, col_near, col_far, out, strip_keep, ends):
    strip_steps(grid, adjoint_steps, edges, grid.ring, STEPS, col_near, col_far, strip_ring, strip_keep, ends)
    for l in range(grid.levels):
        for y in range(grid.rows):
            at = grid.members_at(l, y)
            out[at, :] = control[at, :] + merged(grid, main[l * grid.rows + y], ends[y], l)


def shape_of(*shape):
    return jax.ShapeDtypeStruct(shape, jnp.float32)


def shards(control, perturb, obs_count, obs_weight, diffusivity):
    members, levels, rows, lanes = control.shape
    variables = perturb.shape[1]
    ways = lax.axis_size("mem")
    scale = 1.0 / math.sqrt(members * ways - 1)
    count = members * levels
    grid = Grid(members, levels, rows)
    assert members == SUBLANES and lanes == LANES and grid.block >= 8 * STEPS
    vmem = pl.BlockSpec(memory_space=pltpu.VMEM)
    hbm = pl.BlockSpec(memory_space=pltpu.HBM)
    f32 = jnp.float32

    def call(kernel, *args, work=0, **kwargs):
        cost = pl.CostEstimate(flops=work, bytes_accessed=work, transcendentals=0) if work else None
        return pl.pallas_call(
            lambda *refs: kernel(grid, *refs), compiler_params=PARAMS, cost_estimate=cost, **kwargs
        )(*args)

    def in_hbm(array):
        return pltpu.with_memory_space_constraint(array, pltpu.HBM)

    depth = 2 * STEPS
    ring_shape, strip_shape = (levels * grid.wide, lanes), (grid.padded, lanes)
    rim = shape_of(count * STEPS, lanes)

    def tiles(number):
        return shape_of(number, SUBLANES, lanes)

    edge = tiles(levels * depth + levels + -(-levels * STEPS // SUBLANES))
    level_rows = shape_of(levels * rows, lanes)
    near, far, flat, flat_diff, seen = call(
        rows_kernel,
        in_hbm(control.reshape(count * rows, lanes)),
        in_hbm(diffusivity.reshape(levels * rows, lanes)),
        in_hbm(obs_count.reshape(levels * rows, lanes)),
        out_shape=(edge, edge, shape_of(count * rows, lanes), level_rows, level_rows),
        in_specs=[hbm] * 3,
        scratch_shapes=[pltpu.VMEM(level_rows.shape, jnp.int32), pltpu.SemaphoreType.DMA((3,))],
    )
    got = swap(near, far, "gy")
    edge = tiles(variables * levels * members // 2)
    near, far, held = call(
        perturb_rows_kernel,
        flat_diff,
        in_hbm(perturb),
        work=8 << 20,
        out_shape=(edge, edge, jax.ShapeDtypeStruct(perturb.shape, perturb.dtype)),
        in_specs=[vmem, hbm],
        scratch_shapes=[pltpu.SemaphoreType.DMA((members // 2,))],
    )
    rims = swap(near, far, "gy")
    edge = tiles(grid.wide_packs + 1)
    near, far, edges, ring, ring_edges = call(
        columns_kernel,
        flat,
        flat_diff,
        *got,
        out_shape=(edge, edge, tiles(grid.wide), shape_of(*ring_shape), shape_of(*strip_shape)),
    )
    sides = swap(near, far, "gx")
    main = call(
        spread_main_kernel,
        flat,
        ring,
        *got,
        work=6 << 20,
        out_shape=tiles(levels * grid.ring),
        scratch_shapes=[pltpu.VMEM(ring_shape, f32)],
    )
    piece = -(-variables * levels * grid.ring // (ways * SUBLANES)) * SUBLANES
    partial, strip_ring = call(
        spread_kernel,
        main,
        edges,
        ring_edges,
        *sides,
        held,
        *rims,
        out_shape=(shape_of(ways, piece, lanes), shape_of(*strip_shape)),
        scratch_shapes=[
            pltpu.VMEM(strip_shape, f32),
            pltpu.VMEM((grid.ring, SUBLANES, lanes), f32),
            pltpu.VMEM((count * rows, lanes), f32),
            pltpu.VMEM(rim.shape, f32),
            pltpu.VMEM(rim.shape, f32),
        ],
    )

    parts = lax.all_to_all(partial, "mem", 0, 0)
    mine = jnp.sum(parts, axis=0)
    increment = lax.all_to_all(jnp.broadcast_to(mine, parts.shape), "mem", 0, 0)

    edge = tiles(grid.packs)
    back, before, after, edges, near, far = call(
        lambda grid, *refs: back_kernel(grid, scale, *refs),
        increment,
        seen,
        obs_weight,
        held,
        *rims,
        *got,
        out_shape=(shape_of(count * rows, lanes), rim, rim, tiles(grid.ring), edge, edge),
        in_specs=[vmem, vmem, pl.BlockSpec(memory_space=pltpu.SMEM)] + [vmem] * 5,
    )
    sides = swap(near, far, "gx")
    main = call(
        adjoint_main_kernel,
        back,
        before,
        after,
        ring,
        work=6 << 20,
        out_shape=tiles(levels * rows),
        scratch_shapes=[pltpu.VMEM(ring_shape, f32)],
    )
    out = call(
        adjoint_kernel,
        flat,
        main,
        edges,
        strip_ring,
        *sides,
        out_shape=shape_of(count * rows, lanes),
        scratch_shapes=[pltpu.VMEM(strip_shape, f32), pltpu.VMEM((rows, SUBLANES, lanes), f32)],
    )
    return out.reshape(control.shape)


def solution(mesh):
    placed = (
        P("mem", None, "gy", "gx"),
        P("mem", None, None, "gy", "gx"),
        P(None, "gy", "gx"),
        P(),
        P(None, "gy", "gx"),
    )

    return jax.shard_map(shards, mesh=mesh, in_specs=placed, out_specs=P("mem", None, "gy", "gx"), check_vma=False)
```

time: 76.5 us -> 77 us (level)
  starting transfers between devices: 36.4 us -> 33.4 us
  waiting for transfers between devices: 7.62 us -> 9.64 us
    ppermute x8, starting transfers between devices: 36.4 us -> 33.4 us  [swap(): out.append(lax.ppermute(value, axis, pairs))]
    ppermute x8, waiting for transfers between devices: 7.62 us -> 9.64 us  [swap(): out.append(lax.ppermute(value, axis, pairs))]
    all_to_all x1, blocking collectives: 10.2 us -> 11.3 us  [shards(): increment = lax.all_to_all(jnp.broadcast_to(mine, parts.shape), 'mem', 0, 0)]
    all_to_all x1, blocking collectives: 12.1 us -> 11.3 us  [shards(): parts = lax.all_to_all(partial, 'mem', 0, 0)]
  transfers between devices with their start and end apart: 8 -> 8, of which waited for: 2 -> 3; matrix products, arithmetic and copies ran while one was open for 0% -> 0% of each run, Pallas kernels for 4% -> 4%
where the time goes in v4:
time: 77 us; the launch traced here: 75.5 us
  starting transfers between devices  33.4 us (43%)
  blocking collectives  22.6 us (29%)
  Pallas kernels  9.66 us (13%)
  waiting for transfers between devices  9.64 us (13%)
    ppermute x8, starting transfers between devices, swap(): out.append(lax.ppermute(value, axis, pairs))  33.4 us
    all_to_all x1, blocking collectives, shards(): parts = lax.all_to_all(partial, 'mem', 0, 0)  11.3 us
    all_to_all x1, blocking collectives, shards(): increment = lax.all_to_all(jnp.broadcast_to(mine, parts.shape), 'mem', 0, 0)  11.3 us
    pallas_call x8, Pallas kernels, call(): pl.pallas_call(lambda *refs: kernel(grid, *refs), compiler_params=PARAMS,...  9.66 us
    ppermute x8, waiting for transfers between devices, swap(): out.append(lax.ppermute(value, axis, pairs))  9.64 us
  transfers between devices with their start and end apart: 8, of which 3 were waited for; matrix products, arithmetic and copies ran while one was open for 0% of the time, Pallas kernels for 4%

profile of v4, /device:TPU:24, one launch (start us, length us, event | category | flops | bytes accessed | tf_op | source)
XLA Modules:
  0.0 75.5 jit_solution(3166589941822162922)
XLA Ops:
  0.0 1.2 %shard_map.55 = (f32[29,8,128]{2,1,0:T(8,128)S(1)}, f32[29,8,128]{2,1,0:T(8,128)S(1)}, f32[768,128]{1,0:T(8,128)S(1)}, f32[96,128]{1,0:T(8,128)S(1)}, f32[96,128]{1,0:T(8,128)S(1)}) custom-call(f32[768,128]{1,0:T(8,128)} %bitcast.4, f32[96,128]{1,0:T(8,128)} %bitcast.5, s32[96,128]{1,0:T(8,128)} %bitcast.6), custom_call_target="tpu_custom_call" | custom-call | tf_op jit(solution)/shard_map/pallas_call | solution.py:428
  1.2 1.3 %shard_map.58 = (f32[72,8,128]{2,1,0:T(8,128)S(1)}, f32[72,8,128]{2,1,0:T(8,128)S(1)}, bf16[8,6,3,32,128]{4,3,2,1,0:T(8,128)(2,1)S(1)}) custom-call(f32[96,128]{1,0:T(8,128)S(1)} %get-tuple-element.27.refs_1_.refs_0_, bf16[8,6,3,32,128]{4,3,2,1,0:T(8,128)(2,1)} %refs_1_.1), custom_call_target="tpu_custom_call" | custom-call | flops 8388608 | bytes 8388608 | tf_op jit(solution)/shard_map/pallas_call | solution.py:428
  2.5 2.7 %collective-permute-start.4 = (f32[72,8,128]{2,1,0:T(8,128)S(1)}, f32[72,8,128]{2,1,0:T(8,128)S(1)}, u32[]{:S(2)}, u32[]{:S(2)}) collective-permute-start(f32[72,8,128]{2,1,0:T(8,128)S(1)} %get-tuple-element.36), channel_id=1, source_target_pairs={{0,1},{1,0},{2,3},{3,2},{4,5},{5,4},{6,7},{7,6},{8,9},{9,8},{10,11... | collective-permute-start | bytes 884744 | tf_op jit(solution)/shard_map/ppermute | solution.py:24
  5.2 4.3 %collective-permute-start.5 = (f32[72,8,128]{2,1,0:T(8,128)S(1)}, f32[72,8,128]{2,1,0:T(8,128)S(1)}, u32[]{:S(2)}, u32[]{:S(2)}) collective-permute-start(f32[72,8,128]{2,1,0:T(8,128)S(1)} %get-tuple-element.37), channel_id=1, source_target_pairs={{1,2},{2,1},{3,4},{4,3},{5,6},{6,5},{7,8},{8,7},{9,10},{10,9},{11,... | collective-permute-start | bytes 884744 | tf_op jit(solution)/shard_map/ppermute | solution.py:24
  9.5 5.7 %collective-permute-start = (f32[29,8,128]{2,1,0:T(8,128)S(1)}, f32[29,8,128]{2,1,0:T(8,128)S(1)}, u32[]{:S(2)}, u32[]{:S(2)}) collective-permute-start(f32[29,8,128]{2,1,0:T(8,128)S(1)} %get-tuple-element.28), channel_id=1, source_target_pairs={{0,1},{1,0},{2,3},{3,2},{4,5},{5,4},{6,7},{7,6},{8,9},{9,8},{10,11... | collective-permute-start | bytes 356360 | tf_op jit(solution)/shard_map/ppermute | solution.py:24
  15.2 1.9 %collective-permute-start.1 = (f32[29,8,128]{2,1,0:T(8,128)S(1)}, f32[29,8,128]{2,1,0:T(8,128)S(1)}, u32[]{:S(2)}, u32[]{:S(2)}) collective-permute-start(f32[29,8,128]{2,1,0:T(8,128)S(1)} %get-tuple-element.29), channel_id=1, source_target_pairs={{1,2},{2,1},{3,4},{4,3},{5,6},{6,5},{7,8},{8,7},{9,10},{10,9},{11,... | collective-permute-start | bytes 356360 | tf_op jit(solution)/shard_map/ppermute | solution.py:24
  17.2 0.9 %collective-permute-done.refs_2_.refs_6_ = f32[29,8,128]{2,1,0:T(8,128)S(1)} collective-permute-done((f32[29,8,128]{2,1,0:T(8,128)S(1)}, f32[29,8,128]{2,1,0:T(8,128)S(1)}, u32[]{:S(2)}, u32[]{:S(2)}) %collective-permute-start) | collective-permute-done | bytes 118816 | tf_op jit(solution)/shard_map/ppermute | solution.py:24
  18.0 6.0 %collective-permute-done.1.refs_3_.refs_7_ = f32[29,8,128]{2,1,0:T(8,128)S(1)} collective-permute-done((f32[29,8,128]{2,1,0:T(8,128)S(1)}, f32[29,8,128]{2,1,0:T(8,128)S(1)}, u32[]{:S(2)}, u32[]{:S(2)}) %collective-permute-start.1) | collective-permute-done | bytes 118816 | tf_op jit(solution)/shard_map/ppermute | solution.py:24
  24.1 0.6 shard_map.56
  24.6 5.3 %collective-permute-start.2 = (f32[6,8,128]{2,1,0:T(8,128)S(1)}, f32[6,8,128]{2,1,0:T(8,128)S(1)}, u32[]{:S(2)}, u32[]{:S(2)}) collective-permute-start(f32[6,8,128]{2,1,0:T(8,128)S(1)} %get-tuple-element.33), channel_id=1, source_target_pairs={{0,16},{16,0},{32,48},{48,32},{1,17},{17,1},{33,49},{49,33},{2,18}... | collective-permute-start | bytes 73736 | tf_op jit(solution)/shard_map/ppermute | solution.py:24
  29.9 0.7 collective-permute-start.3
  30.6 1.2 %shard_map.57.refs_0_ = f32[120,8,128]{2,1,0:T(8,128)S(1)} custom-call(f32[768,128]{1,0:T(8,128)S(1)} %get-tuple-element.26.refs_0_, f32[144,128]{1,0:T(8,128)S(1)} %get-tuple-element.30.refs_1_.refs_3_, f32[29,8,128]{2,1,0:T(8,128)S(1)} %collective-permute-done.refs_2_.refs_6_, f32[29,8,128]{2,1,0:T(8,128)S(1)} %collective-permute-done.1.refs_3_.refs_7_), custom_call_target="tpu_custom_call" | custom-call | flops 6291456 | bytes 6291456 | tf_op jit(solution)/shard_map/pallas_call | solution.py:428
  31.8 2.7 %collective-permute-done.2.refs_3_ = f32[6,8,128]{2,1,0:T(8,128)S(1)} collective-permute-done((f32[6,8,128]{2,1,0:T(8,128)S(1)}, f32[6,8,128]{2,1,0:T(8,128)S(1)}, u32[]{:S(2)}, u32[]{:S(2)}) %collective-permute-start.2) | collective-permute-done | bytes 24608 | tf_op jit(solution)/shard_map/ppermute | solution.py:24
  34.5 0.0 collective-permute-done.3.refs_4_
  34.5 0.0 collective-permute-done.4.refs_6_.refs_4_
  34.5 0.0 collective-permute-done.5.refs_7_.refs_5_
  34.5 1.3 %shard_map.59 = (f32[8,96,128]{2,1,0:T(8,128)S(1)}, f32[56,128]{1,0:T(8,128)S(1)}) custom-call(f32[120,8,128]{2,1,0:T(8,128)S(1)} %shard_map.57.refs_0_, f32[48,8,128]{2,1,0:T(8,128)S(1)} %get-tuple-element.31.refs_1_, f32[56,128]{1,0:T(8,128)S(1)} %get-tuple-element.32.refs_2_, f32[6,8,128]{2,1,0:T(8,128)S(1)} %collective-permute-done.2.refs_3_, ...), custom_call_target="tpu_custom_call" | custom-call | tf_op jit(solution)/shard_map/pallas_call | solution.py:428
  35.9 0.0 copy-start
  35.9 11.3 %all_to_all.10 = f32[8,96,128]{2,1,0:T(8,128)S(1)} all-to-all(f32[8,96,128]{2,1,0:T(8,128)S(1)} %get-tuple-element.38), channel_id=1, replica_groups=mesh['mem'=8,'gx'=4,'gy'=16] {'mem'}, dimensions={0} | all-to-all | bytes 786432 | tf_op jit(solution)/shard_map/all_to_all | solution.py:502
  47.2 11.3 %all_to_all.11.refs_0_ = f32[8,96,128]{2,1,0:T(8,128)S(1)} all-to-all(f32[8,96,128]{2,1,0:T(8,128)S(1)} %broadcast_in_dim.3), channel_id=1, replica_groups=mesh['mem'=8,'gx'=4,'gy'=16] {'mem'}, dimensions={0} | all-to-all | bytes 786432 | tf_op jit(solution)/shard_map/all_to_all | solution.py:504
  58.5 0.0 copy-done
  58.5 1.3 %shard_map.60 = (f32[768,128]{1,0:T(8,128)S(1)}, f32[96,128]{1,0:T(8,128)S(1)}, f32[96,128]{1,0:T(8,128)S(1)}, f32[40,8,128]{2,1,0:T(8,128)S(1)}, f32[4,8,128]{2,1,0:T(8,128)S(1)}, /*index=5*/f32[4,8,128]{2,1,0:T(8,128)S(1)}) custom-call(f32[8,96,128]{2,1,0:T(8,128)S(1)} %all_to_all.11.refs_0_, f32[96,128]{1,0:T(8,128)S(1)} %get-tuple-element.39.refs_1_, ...), custom_call_target="tpu_custom_call" | custom-call | tf_op jit(solution)/shard_map/pallas_call | solution.py:428
  59.8 12.2 %collective-permute-start.6 = (f32[4,8,128]{2,1,0:T(8,128)S(1)}, f32[4,8,128]{2,1,0:T(8,128)S(1)}, u32[]{:S(2)}, u32[]{:S(2)}) collective-permute-start(f32[4,8,128]{2,1,0:T(8,128)S(1)} %get-tuple-element.45), channel_id=1, source_target_pairs={{0,16},{16,0},{32,48},{48,32},{1,17},{17,1},{33,49},{49,33},{2,18}... | collective-permute-start | bytes 49160 | tf_op jit(solution)/shard_map/ppermute | solution.py:24
  72.1 0.7 collective-permute-start.7
  72.7 1.0 %shard_map.61.refs_1_ = f32[96,8,128]{2,1,0:T(8,128)S(1)} custom-call(f32[768,128]{1,0:T(8,128)S(1)} %get-tuple-element.40.refs_0_, f32[96,128]{1,0:T(8,128)S(1)} %get-tuple-element.41.refs_1_, f32[96,128]{1,0:T(8,128)S(1)} %get-tuple-element.42.refs_2_, f32[144,128]{1,0:T(8,128)S(1)} %get-tuple-element.30.refs_1_.refs_3_), custom_call_target="tpu_custom_call" | custom-call | flops 6291456 | bytes 6291456 | tf_op jit(solution)/shard_map/pallas_call | solution.py:428
  73.8 0.0 collective-permute-done.6.refs_4_
  73.8 0.0 collective-permute-done.7.refs_5_
  73.8 1.7 %shard_map.62 = f32[768,128]{1,0:T(8,128)} custom-call(f32[768,128]{1,0:T(8,128)S(1)} %get-tuple-element.26.refs_0_, f32[96,8,128]{2,1,0:T(8,128)S(1)} %shard_map.61.refs_1_, f32[40,8,128]{2,1,0:T(8,128)S(1)} %get-tuple-element.43.refs_2_, f32[56,128]{1,0:T(8,128)S(1)} %get-tuple-element.44.refs_3_, f32[4,8,128]{2,1,0:T(8,128)S(1)} %collective-permute-done.6.refs_4_, ...), custom_call_target="tpu_custom_call" | custom-call | tf_op jit(solution)/shard_map/pallas_call | solution.py:428
  (2 shorter events, 0.1 us)
Async XLA Ops:
  2.5 32.0 %collective-permute-start.4 = (f32[72,8,128]{2,1,0:T(8,128)S(1)}, f32[72,8,128]{2,1,0:T(8,128)S(1)}, u32[]{:S(2)}, u32[]{:S(2)}) collective-permute-start(f32[72,8,128]{2,1,0:T(8,128)S(1)} %get-tuple-element.36), channel_id=1, source_target_pairs={{0,1},{1,0},{2,3},{3,2},{4,5},{5,4},{6,7},{7,6},{8,9},{9,8},{10,11... | collective-permute-start | bytes 884744 | tf_op jit(solution)/shard_map/ppermute | solution.py:24
  5.2 29.4 %collective-permute-start.5 = (f32[72,8,128]{2,1,0:T(8,128)S(1)}, f32[72,8,128]{2,1,0:T(8,128)S(1)}, u32[]{:S(2)}, u32[]{:S(2)}) collective-permute-start(f32[72,8,128]{2,1,0:T(8,128)S(1)} %get-tuple-element.37), channel_id=1, source_target_pairs={{1,2},{2,1},{3,4},{4,3},{5,6},{6,5},{7,8},{8,7},{9,10},{10,9},{11,... | collective-permute-start | bytes 884744 | tf_op jit(solution)/shard_map/ppermute | solution.py:24
  9.5 8.6 %collective-permute-start = (f32[29,8,128]{2,1,0:T(8,128)S(1)}, f32[29,8,128]{2,1,0:T(8,128)S(1)}, u32[]{:S(2)}, u32[]{:S(2)}) collective-permute-start(f32[29,8,128]{2,1,0:T(8,128)S(1)} %get-tuple-element.28), channel_id=1, source_target_pairs={{0,1},{1,0},{2,3},{3,2},{4,5},{5,4},{6,7},{7,6},{8,9},{9,8},{10,11... | collective-permute-start | bytes 356360 | tf_op jit(solution)/shard_map/ppermute | solution.py:24
  15.2 8.8 %collective-permute-start.1 = (f32[29,8,128]{2,1,0:T(8,128)S(1)}, f32[29,8,128]{2,1,0:T(8,128)S(1)}, u32[]{:S(2)}, u32[]{:S(2)}) collective-permute-start(f32[29,8,128]{2,1,0:T(8,128)S(1)} %get-tuple-element.29), channel_id=1, source_target_pairs={{1,2},{2,1},{3,4},{4,3},{5,6},{6,5},{7,8},{8,7},{9,10},{10,9},{11,... | collective-permute-start | bytes 356360 | tf_op jit(solution)/shard_map/ppermute | solution.py:24
  24.6 9.9 %collective-permute-start.2 = (f32[6,8,128]{2,1,0:T(8,128)S(1)}, f32[6,8,128]{2,1,0:T(8,128)S(1)}, u32[]{:S(2)}, u32[]{:S(2)}) collective-permute-start(f32[6,8,128]{2,1,0:T(8,128)S(1)} %get-tuple-element.33), channel_id=1, source_target_pairs={{0,16},{16,0},{32,48},{48,32},{1,17},{17,1},{33,49},{49,33},{2,18}... | collective-permute-start | bytes 73736 | tf_op jit(solution)/shard_map/ppermute | solution.py:24
  29.9 4.6 %collective-permute-start.3 = (f32[6,8,128]{2,1,0:T(8,128)S(1)}, f32[6,8,128]{2,1,0:T(8,128)S(1)}, u32[]{:S(2)}, u32[]{:S(2)}) collective-permute-start(f32[6,8,128]{2,1,0:T(8,128)S(1)} %get-tuple-element.34), channel_id=1, source_target_pairs={{16,32},{32,16},{17,33},{33,17},{18,34},{34,18},{19,35},{35,19},{2... | collective-permute-start | bytes 73736 | tf_op jit(solution)/shard_map/ppermute | solution.py:24
  35.9 22.7 %copy-start = (f32[6]{0:T(128)S(1)}, f32[6]{0:T(128)}, u32[]{:S(2)}) copy-start(f32[6]{0:T(128)} %refs_2_.1) | copy-start | bytes 76
  59.8 13.9 %collective-permute-start.6 = (f32[4,8,128]{2,1,0:T(8,128)S(1)}, f32[4,8,128]{2,1,0:T(8,128)S(1)}, u32[]{:S(2)}, u32[]{:S(2)}) collective-permute-start(f32[4,8,128]{2,1,0:T(8,128)S(1)} %get-tuple-element.45), channel_id=1, source_target_pairs={{0,16},{16,0},{32,48},{48,32},{1,17},{17,1},{33,49},{49,33},{2,18}... | collective-permute-start | bytes 49160 | tf_op jit(solution)/shard_map/ppermute | solution.py:24
  72.1 1.7 %collective-permute-start.7 = (f32[4,8,128]{2,1,0:T(8,128)S(1)}, f32[4,8,128]{2,1,0:T(8,128)S(1)}, u32[]{:S(2)}, u32[]{:S(2)}) collective-permute-start(f32[4,8,128]{2,1,0:T(8,128)S(1)} %get-tuple-element.46), channel_id=1, source_target_pairs={{16,32},{32,16},{17,33},{33,17},{18,34},{34,18},{19,35},{35,19},{2... | collective-permute-start | bytes 49160 | tf_op jit(solution)/shard_map/ppermute | solution.py:24

commit v5 on v4

--- a/solution.py
+++ b/solution.py
@@ -152,17 +152,23 @@
     return lambda k: jnp.broadcast_to(ref[pl.ds(start + k, 1), :], (SUBLANES, LANES))
 
 
-def rows_kernel(grid, control_hbm, diffusivity_hbm, count_hbm, near, far, control, diffusivity, seen, count, sems):
+def rows_kernel(
+    grid, control_hbm, diffusivity_hbm, count_hbm, weight_hbm, near, far, control, diffusivity, seen, weights, count, weight, sems
+):
     levels, rows = grid.levels, grid.rows
     depth = 2 * STEPS
     copies = [
         pltpu.make_async_copy(diffusivity_hbm, diffusivity, sems.at[0]),
         pltpu.make_async_copy(count_hbm, count, sems.at[1]),
         pltpu.make_async_copy(control_hbm, control, sems.at[2]),
+        pltpu.make_async_copy(weight_hbm, weight, sems.at[3]),
     ]
     for copy in copies:
         copy.start()
     odd = is_odd("gy")
+    copies[3].wait()
+    for v in range(weights.shape[0]):
+        weights[v] = jnp.full((SUBLANES, LANES), weight[v])
     copies[0].wait()
     copies[1].wait()
     seen[...] = count[...].astype(jnp.float32)
@@ -193,23 +199,24 @@
     return lax.broadcasted_iota(jnp.int32, (SUBLANES, LANES), 0) < STEPS
 
 
-def perturb_rows_kernel(grid, order, perturb_hbm, near, far, perturb, sems):
-    members, variables, levels, rows, _ = perturb.shape
+def perturb_rows_kernel(grid, order, perturb_hbm, near, far, heads, tails, sems):
+    members, variables, levels, rows, _ = perturb_hbm.shape
     copies = [
-        pltpu.make_async_copy(perturb_hbm.at[pl.ds(2 * q, 2)], perturb.at[pl.ds(2 * q, 2)], sems.at[q]) for q in range(members // 2)
+        pltpu.make_async_copy(perturb_hbm.at[:, :, :, pl.ds(0, SUBLANES), :], heads, sems.at[0]),
+        pltpu.make_async_copy(perturb_hbm.at[:, :, :, pl.ds(rows - SUBLANES, SUBLANES), :], tails, sems.at[1]),
     ]
     for copy in copies:
         copy.start()
+    for copy in copies:
+        copy.wait()
     odd = is_odd("gy")
-    tile = 2 * SUBLANES
-    for q, copy in enumerate(copies):
-        copy.wait()
+    for q in range(members // 2):
         for v in range(variables):
             for l in range(levels):
-                heads = [perturb[2 * q + j, v, l, :tile, :].astype(jnp.float32)[:SUBLANES] for j in range(2)]
-                tails = [perturb[2 * q + j, v, l, rows - tile :, :].astype(jnp.float32)[SUBLANES:] for j in range(2)]
-                first = jnp.where(upper(), heads[0], turned(heads[1]))
-                last = jnp.where(upper(), turned(tails[0]), tails[1])
+                head = [heads[2 * q + j, v, l].astype(jnp.float32) for j in range(2)]
+                tail = [tails[2 * q + j, v, l].astype(jnp.float32) for j in range(2)]
+                first = jnp.where(upper(), head[0], turned(head[1]))
+                last = jnp.where(upper(), turned(tail[0]), tail[1])
                 at = (v * levels + l) * (members // 2) + q
                 near[at], far[at] = ordered(odd, first, last)
 
@@ -244,7 +251,9 @@
     far[packs, :packs, :] = b
 
 
-def spread_main_kernel(grid, control, ring, got_near, got_far, main, keep):
+def spread_main_kernel(grid, control, ring, got_near, got_far, perturb_hbm, main, perturb, keep, sem):
+    copy = pltpu.make_async_copy(perturb_hbm, perturb, sem)
+    copy.start()
     odd = is_odd("gy")
     keep[...] = 1.0 - 4.0 * ring[...]
     for l in range(grid.levels):
@@ -252,6 +261,7 @@
         at = l * grid.wide
         for y, row in enumerate(spread_steps(rows, row_reader(ring, at), row_reader(keep, at))):
             main[l * grid.ring + y] = row
+    copy.wait()
 
 
 def adjoint_main_kernel(grid, back, before, after, ring, main, keep):
@@ -348,7 +358,7 @@
     scale,
     increment,
     seen,
-    obs_weight,
+    weights,
     perturb,
     rim_near,
     rim_far,
@@ -371,7 +381,8 @@
             weighted = []
             for v in range(variables):
                 at = [grid.tile_of(increment, v * levels + l, start // SUBLANES + j) for j in range(2)]
-                weighted.append(factor * obs_weight[v] * jnp.concatenate([increment[at[0]], increment[at[1]]], axis=0))
+                pair = [weights[v] * increment[a] for a in at]
+                weighted.append(factor * jnp.concatenate(pair, axis=0))
             for m in range(members):
                 total = perturb[m, 0, l, start : start + tile, :].astype(jnp.float32) * weighted[0]
                 for v in range(1, variables):
@@ -387,7 +398,7 @@
             both = increment[grid.tile_of(increment, v * levels + l, rows // SUBLANES)]
             after = jnp.where(upper(), both, turned(both))
             before = jnp.where(upper(), turned(both), both)
-            weighted = [c * obs_weight[v] * w for c, w in zip(counts, (after, before))]
+            weighted = [c * (weights[v] * w) for c, w in zip(counts, (after, before))]
             for q in range(pairs):
                 at = (v * levels + l) * pairs + q
                 for side, p in enumerate(ordered(odd, rim_far[at], rim_near[at])):
@@ -399,12 +410,20 @@
     field_columns(grid, lambda l, k: grid.ring_row(back, back_before, back_after, l, k), grid.ring, near, far, edges)
 
 
-def adjoint_kernel(grid, control, main, edges, strip_ring, col_near, col_far, out, strip_keep, ends):
+def adjoint_kernel(grid, control, main, edges, strip_ring, col_near, col_far, out_hbm, strip_keep, ends, out, sems):
     strip_steps(grid, adjoint_steps, edges, grid.ring, STEPS, col_near, col_far, strip_ring, strip_keep, ends)
-    for l in range(grid.levels):
-        for y in range(grid.rows):
-            at = grid.members_at(l, y)
-            out[at, :] = control[at, :] + merged(grid, main[l * grid.rows + y], ends[y], l)
+    planes = (grid.members * grid.levels, grid.rows, LANES)
+    copies = []
+    for start in range(0, grid.rows, SUBLANES):
+        for l in range(grid.levels):
+            for y in range(start, start + SUBLANES):
+                at = grid.members_at(l, y)
+                out[at, :] = control[at, :] + merged(grid, main[l * grid.rows + y], ends[y], l)
+        part = pl.ds(start, SUBLANES)
+        copies.append(pltpu.make_async_copy(out.reshape(planes).at[:, part, :], out_hbm.at[:, part, :], sems.at[start // SUBLANES]))
+        copies[-1].start()
+    for copy in copies:
+        copy.wait()
 
 
 def shape_of(*shape):
@@ -441,25 +460,31 @@
 
     edge = tiles(levels * depth + levels + -(-levels * STEPS // SUBLANES))
     level_rows = shape_of(levels * rows, lanes)
-    near, far, flat, flat_diff, seen = call(
+    near, far, flat, flat_diff, seen, weights = call(
         rows_kernel,
         in_hbm(control.reshape(count * rows, lanes)),
         in_hbm(diffusivity.reshape(levels * rows, lanes)),
         in_hbm(obs_count.reshape(levels * rows, lanes)),
-        out_shape=(edge, edge, shape_of(count * rows, lanes), level_rows, level_rows),
-        in_specs=[hbm] * 3,
-        scratch_shapes=[pltpu.VMEM(level_rows.shape, jnp.int32), pltpu.SemaphoreType.DMA((3,))],
+        in_hbm(obs_weight),
+        out_shape=(edge, edge, shape_of(count * rows, lanes), level_rows, level_rows, tiles(variables)),
+        in_specs=[hbm] * 4,
+        scratch_shapes=[
+            pltpu.VMEM(level_rows.shape, jnp.int32),
+            pltpu.SMEM(obs_weight.shape, f32),
+            pltpu.SemaphoreType.DMA((4,)),
+        ],
     )
     got = swap(near, far, "gy")
     edge = tiles(variables * levels * members // 2)
-    near, far, held = call(
+    edge_rows = pltpu.VMEM((members, variables, levels, SUBLANES, lanes), perturb.dtype)
+    near, far = call(
         perturb_rows_kernel,
         flat_diff,
         in_hbm(perturb),
         work=8 << 20,
-        out_shape=(edge, edge, jax.ShapeDtypeStruct(perturb.shape, perturb.dtype)),
+        out_shape=(edge, edge),
         in_specs=[vmem, hbm],
-        scratch_shapes=[pltpu.SemaphoreType.DMA((members // 2,))],
+        scratch_shapes=[edge_rows, edge_rows, pltpu.SemaphoreType.DMA((2,))],
     )
     rims = swap(near, far, "gy")
     edge = tiles(grid.wide_packs + 1)
@@ -471,14 +496,16 @@
         out_shape=(edge, edge, tiles(grid.wide), shape_of(*ring_shape), shape_of(*strip_shape)),
     )
     sides = swap(near, far, "gx")
-    main = call(
+    main, held = call(
         spread_main_kernel,
         flat,
         ring,
         *got,
+        in_hbm(perturb),
         work=6 << 20,
-        out_shape=tiles(levels * grid.ring),
-        scratch_shapes=[pltpu.VMEM(ring_shape, f32)],
+        out_shape=(tiles(levels * grid.ring), jax.ShapeDtypeStruct(perturb.shape, perturb.dtype)),
+        in_specs=[vmem] * 4 + [hbm],
+        scratch_shapes=[pltpu.VMEM(ring_shape, f32), pltpu.SemaphoreType.DMA],
     )
     piece = -(-variables * levels * grid.ring // (ways * SUBLANES)) * SUBLANES
     partial, strip_ring = call(
@@ -508,12 +535,11 @@
         lambda grid, *refs: back_kernel(grid, scale, *refs),
         increment,
         seen,
-        obs_weight,
+        weights,
         held,
         *rims,
         *got,
         out_shape=(shape_of(count * rows, lanes), rim, rim, tiles(grid.ring), edge, edge),
-        in_specs=[vmem, vmem, pl.BlockSpec(memory_space=pltpu.SMEM)] + [vmem] * 5,
     )
     sides = swap(near, far, "gx")
     main = call(
@@ -533,8 +559,14 @@
         edges,
         strip_ring,
         *sides,
-        out_shape=shape_of(count * rows, lanes),
-        scratch_shapes=[pltpu.VMEM(strip_shape, f32), pltpu.VMEM((rows, SUBLANES, lanes), f32)],
+        out_shape=shape_of(count, rows, lanes),
+        out_specs=hbm,
+        scratch_shapes=[
+            pltpu.VMEM(strip_shape, f32),
+            pltpu.VMEM((rows, SUBLANES, lanes), f32),
+            pltpu.VMEM((count * rows, lanes), f32),
+            pltpu.SemaphoreType.DMA((rows // SUBLANES,)),
+        ],
     )
     return out.reshape(control.shape)
 

time: 77 us -> 76.4 us (level)
  the two profiles are of different devices: /device:TPU:24 before, /device:TPU:160 now
where the time goes in v5:
time: 76.4 us; the launch traced here: 75.9 us
  starting transfers between devices  35.6 us (47%)
  blocking collectives  24.3 us (32%)
  Pallas kernels  9.03 us (12%)
  waiting for transfers between devices  6.81 us (9%)
    ppermute x8, starting transfers between devices, swap(): out.append(lax.ppermute(value, axis, pairs))  35.6 us
    all_to_all x1, blocking collectives, shards(): parts = lax.all_to_all(partial, 'mem', 0, 0)  13 us
    all_to_all x1, blocking collectives, shards(): increment = lax.all_to_all(jnp.broadcast_to(mine, parts.shape), 'mem', 0, 0)  11.3 us
    pallas_call x8, Pallas kernels, call(): pl.pallas_call(lambda *refs: kernel(grid, *refs), compiler_params=PARAMS,...  9.03 us
    ppermute x8, waiting for transfers between devices, swap(): out.append(lax.ppermute(value, axis, pairs))  6.81 us
  transfers between devices with their start and end apart: 8, of which 4 were waited for; matrix products, arithmetic and copies ran while one was open for 0% of the time, Pallas kernels for 4%

profile of v5, /device:TPU:160, one launch (start us, length us, event | category | flops | bytes accessed | tf_op | source)
XLA Modules:
  0.0 75.9 jit_solution(2569847390977051064)
XLA Ops:
  0.0 1.2 %shard_map.55 = (f32[29,8,128]{2,1,0:T(8,128)S(1)}, f32[29,8,128]{2,1,0:T(8,128)S(1)}, f32[768,128]{1,0:T(8,128)S(1)}, f32[96,128]{1,0:T(8,128)S(1)}, f32[96,128]{1,0:T(8,128)S(1)}, /*index=5*/f32[6,8,128]{2,1,0:T(8,128)S(1)}) custom-call(f32[768,128]{1,0:T(8,128)} %bitcast.4, f32[96,128]{1,0:T(8,128)} %bitcast.5, s32[96,128]{1,0:T(8,128)} %bitcast.6, f32[6]{0:T(128)} %refs_3_.1), custom_call_target="tpu_custom_call" | custom-call | tf_op jit(solution)/shard_map/pallas_call | solution.py:447
  1.2 1.2 %shard_map.58 = (f32[72,8,128]{2,1,0:T(8,128)S(1)}, f32[72,8,128]{2,1,0:T(8,128)S(1)}) custom-call(f32[96,128]{1,0:T(8,128)S(1)} %get-tuple-element.29.refs_1_.refs_0_, bf16[8,6,3,32,128]{4,3,2,1,0:T(8,128)(2,1)} %refs_1_.1), custom_call_target="tpu_custom_call" | custom-call | flops 8388608 | bytes 8388608 | tf_op jit(solution)/shard_map/pallas_call | solution.py:447
  2.4 3.5 %collective-permute-start.4 = (f32[72,8,128]{2,1,0:T(8,128)S(1)}, f32[72,8,128]{2,1,0:T(8,128)S(1)}, u32[]{:S(2)}, u32[]{:S(2)}) collective-permute-start(f32[72,8,128]{2,1,0:T(8,128)S(1)} %get-tuple-element.39), channel_id=1, source_target_pairs={{0,1},{1,0},{2,3},{3,2},{4,5},{5,4},{6,7},{7,6},{8,9},{9,8},{10,11... | collective-permute-start | bytes 884744 | tf_op jit(solution)/shard_map/ppermute | solution.py:24
  5.9 3.6 %collective-permute-start.5 = (f32[72,8,128]{2,1,0:T(8,128)S(1)}, f32[72,8,128]{2,1,0:T(8,128)S(1)}, u32[]{:S(2)}, u32[]{:S(2)}) collective-permute-start(f32[72,8,128]{2,1,0:T(8,128)S(1)} %get-tuple-element.40), channel_id=1, source_target_pairs={{1,2},{2,1},{3,4},{4,3},{5,6},{6,5},{7,8},{8,7},{9,10},{10,9},{11,... | collective-permute-start | bytes 884744 | tf_op jit(solution)/shard_map/ppermute | solution.py:24
  9.5 3.0 %collective-permute-start = (f32[29,8,128]{2,1,0:T(8,128)S(1)}, f32[29,8,128]{2,1,0:T(8,128)S(1)}, u32[]{:S(2)}, u32[]{:S(2)}) collective-permute-start(f32[29,8,128]{2,1,0:T(8,128)S(1)} %get-tuple-element.30), channel_id=1, source_target_pairs={{0,1},{1,0},{2,3},{3,2},{4,5},{5,4},{6,7},{7,6},{8,9},{9,8},{10,11... | collective-permute-start | bytes 356360 | tf_op jit(solution)/shard_map/ppermute | solution.py:24
  12.6 3.2 %collective-permute-start.1 = (f32[29,8,128]{2,1,0:T(8,128)S(1)}, f32[29,8,128]{2,1,0:T(8,128)S(1)}, u32[]{:S(2)}, u32[]{:S(2)}) collective-permute-start(f32[29,8,128]{2,1,0:T(8,128)S(1)} %get-tuple-element.31), channel_id=1, source_target_pairs={{1,2},{2,1},{3,4},{4,3},{5,6},{6,5},{7,8},{8,7},{9,10},{10,9},{11,... | collective-permute-start | bytes 356360 | tf_op jit(solution)/shard_map/ppermute | solution.py:24
  15.8 0.5 collective-permute-done.refs_2_.refs_6_
  16.3 5.2 %collective-permute-done.1.refs_3_.refs_7_ = f32[29,8,128]{2,1,0:T(8,128)S(1)} collective-permute-done((f32[29,8,128]{2,1,0:T(8,128)S(1)}, f32[29,8,128]{2,1,0:T(8,128)S(1)}, u32[]{:S(2)}, u32[]{:S(2)}) %collective-permute-start.1) | collective-permute-done | bytes 118816 | tf_op jit(solution)/shard_map/ppermute | solution.py:24
  21.4 0.6 shard_map.56
  22.0 1.9 %collective-permute-start.2 = (f32[6,8,128]{2,1,0:T(8,128)S(1)}, f32[6,8,128]{2,1,0:T(8,128)S(1)}, u32[]{:S(2)}, u32[]{:S(2)}) collective-permute-start(f32[6,8,128]{2,1,0:T(8,128)S(1)} %get-tuple-element.36), channel_id=1, source_target_pairs={{0,16},{16,0},{32,48},{48,32},{1,17},{17,1},{33,49},{49,33},{2,18}... | collective-permute-start | bytes 73736 | tf_op jit(solution)/shard_map/ppermute | solution.py:24
  23.9 10.6 %collective-permute-start.3 = (f32[6,8,128]{2,1,0:T(8,128)S(1)}, f32[6,8,128]{2,1,0:T(8,128)S(1)}, u32[]{:S(2)}, u32[]{:S(2)}) collective-permute-start(f32[6,8,128]{2,1,0:T(8,128)S(1)} %get-tuple-element.37), channel_id=1, source_target_pairs={{16,32},{32,16},{17,33},{33,17},{18,34},{34,18},{19,35},{35,19},{2... | collective-permute-start | bytes 73736 | tf_op jit(solution)/shard_map/ppermute | solution.py:24
  34.5 1.3 %shard_map.57 = (f32[120,8,128]{2,1,0:T(8,128)S(1)}, bf16[8,6,3,32,128]{4,3,2,1,0:T(8,128)(2,1)S(1)}) custom-call(f32[768,128]{1,0:T(8,128)S(1)} %get-tuple-element.28.refs_0_, f32[144,128]{1,0:T(8,128)S(1)} %get-tuple-element.32.refs_1_.refs_3_, f32[29,8,128]{2,1,0:T(8,128)S(1)} %collective-permute-done.refs_2_.refs_6_, ...), custom_call_target="tpu_custom_call" | custom-call | flops 6291456 | bytes 6291456 | tf_op jit(solution)/shard_map/pallas_call | solution.py:447
  35.8 0.0 collective-permute-done.2.refs_3_
  35.8 0.5 collective-permute-done.3.refs_4_
  36.3 0.0 collective-permute-done.4.refs_6_.refs_4_
  36.3 0.0 collective-permute-done.5.refs_7_.refs_5_
  36.3 1.3 %shard_map.59 = (f32[8,96,128]{2,1,0:T(8,128)S(1)}, f32[56,128]{1,0:T(8,128)S(1)}) custom-call(f32[120,8,128]{2,1,0:T(8,128)S(1)} %get-tuple-element.33.refs_0_, f32[48,8,128]{2,1,0:T(8,128)S(1)} %get-tuple-element.34.refs_1_, f32[56,128]{1,0:T(8,128)S(1)} %get-tuple-element.35.refs_2_, f32[6,8,128]{2,1,0:T(8,128)S(1)} %collective-permute-done.2.refs_3_, ...), custom_call_target="tpu_custom_call" | custom-call | tf_op jit(solution)/shard_map/pallas_call | solution.py:447
  37.6 13.0 %all_to_all.10 = f32[8,96,128]{2,1,0:T(8,128)S(1)} all-to-all(f32[8,96,128]{2,1,0:T(8,128)S(1)} %get-tuple-element.41), channel_id=1, replica_groups=mesh['mem'=8,'gx'=4,'gy'=16] {'mem'}, dimensions={0} | all-to-all | bytes 786432 | tf_op jit(solution)/shard_map/all_to_all | solution.py:529
  50.7 11.3 %all_to_all.11.refs_0_ = f32[8,96,128]{2,1,0:T(8,128)S(1)} all-to-all(f32[8,96,128]{2,1,0:T(8,128)S(1)} %broadcast_in_dim.3), channel_id=1, replica_groups=mesh['mem'=8,'gx'=4,'gy'=16] {'mem'}, dimensions={0} | all-to-all | bytes 786432 | tf_op jit(solution)/shard_map/all_to_all | solution.py:531
  62.0 0.8 shard_map.60
  62.8 1.9 %collective-permute-start.6 = (f32[4,8,128]{2,1,0:T(8,128)S(1)}, f32[4,8,128]{2,1,0:T(8,128)S(1)}, u32[]{:S(2)}, u32[]{:S(2)}) collective-permute-start(f32[4,8,128]{2,1,0:T(8,128)S(1)} %get-tuple-element.49), channel_id=1, source_target_pairs={{0,16},{16,0},{32,48},{48,32},{1,17},{17,1},{33,49},{49,33},{2,18}... | collective-permute-start | bytes 49160 | tf_op jit(solution)/shard_map/ppermute | solution.py:24
  64.7 7.8 %collective-permute-start.7 = (f32[4,8,128]{2,1,0:T(8,128)S(1)}, f32[4,8,128]{2,1,0:T(8,128)S(1)}, u32[]{:S(2)}, u32[]{:S(2)}) collective-permute-start(f32[4,8,128]{2,1,0:T(8,128)S(1)} %get-tuple-element.50), channel_id=1, source_target_pairs={{16,32},{32,16},{17,33},{33,17},{18,34},{34,18},{19,35},{35,19},{2... | collective-permute-start | bytes 49160 | tf_op jit(solution)/shard_map/ppermute | solution.py:24
  72.5 1.0 %shard_map.61.refs_1_ = f32[96,8,128]{2,1,0:T(8,128)S(1)} custom-call(f32[768,128]{1,0:T(8,128)S(1)} %get-tuple-element.44.refs_0_, f32[96,128]{1,0:T(8,128)S(1)} %get-tuple-element.45.refs_1_, f32[96,128]{1,0:T(8,128)S(1)} %get-tuple-element.46.refs_2_, f32[144,128]{1,0:T(8,128)S(1)} %get-tuple-element.32.refs_1_.refs_3_), custom_call_target="tpu_custom_call" | custom-call | flops 6291456 | bytes 6291456 | tf_op jit(solution)/shard_map/pallas_call | solution.py:447
  73.6 0.0 collective-permute-done.6.refs_4_
  73.6 0.7 collective-permute-done.7.refs_5_
  74.3 1.7 %shard_map.62 = f32[24,32,128]{2,1,0:T(8,128)} custom-call(f32[768,128]{1,0:T(8,128)S(1)} %get-tuple-element.28.refs_0_, f32[96,8,128]{2,1,0:T(8,128)S(1)} %shard_map.61.refs_1_, f32[40,8,128]{2,1,0:T(8,128)S(1)} %get-tuple-element.47.refs_2_, f32[56,128]{1,0:T(8,128)S(1)} %get-tuple-element.48.refs_3_, f32[4,8,128]{2,1,0:T(8,128)S(1)} %collective-permute-done.6.refs_4_, ...), custom_call_target="tpu_custom_call" | custom-call | tf_op jit(solution)/shard_map/pallas_call | solution.py:447
  (2 shorter events, 0.1 us)
Async XLA Ops:
  2.4 33.9 %collective-permute-start.4 = (f32[72,8,128]{2,1,0:T(8,128)S(1)}, f32[72,8,128]{2,1,0:T(8,128)S(1)}, u32[]{:S(2)}, u32[]{:S(2)}) collective-permute-start(f32[72,8,128]{2,1,0:T(8,128)S(1)} %get-tuple-element.39), channel_id=1, source_target_pairs={{0,1},{1,0},{2,3},{3,2},{4,5},{5,4},{6,7},{7,6},{8,9},{9,8},{10,11... | collective-permute-start | bytes 884744 | tf_op jit(solution)/shard_map/ppermute | solution.py:24
  5.9 30.4 %collective-permute-start.5 = (f32[72,8,128]{2,1,0:T(8,128)S(1)}, f32[72,8,128]{2,1,0:T(8,128)S(1)}, u32[]{:S(2)}, u32[]{:S(2)}) collective-permute-start(f32[72,8,128]{2,1,0:T(8,128)S(1)} %get-tuple-element.40), channel_id=1, source_target_pairs={{1,2},{2,1},{3,4},{4,3},{5,6},{6,5},{7,8},{8,7},{9,10},{10,9},{11,... | collective-permute-start | bytes 884744 | tf_op jit(solution)/shard_map/ppermute | solution.py:24
  9.5 6.7 %collective-permute-start = (f32[29,8,128]{2,1,0:T(8,128)S(1)}, f32[29,8,128]{2,1,0:T(8,128)S(1)}, u32[]{:S(2)}, u32[]{:S(2)}) collective-permute-start(f32[29,8,128]{2,1,0:T(8,128)S(1)} %get-tuple-element.30), channel_id=1, source_target_pairs={{0,1},{1,0},{2,3},{3,2},{4,5},{5,4},{6,7},{7,6},{8,9},{9,8},{10,11... | collective-permute-start | bytes 356360 | tf_op jit(solution)/shard_map/ppermute | solution.py:24
  12.6 8.8 %collective-permute-start.1 = (f32[29,8,128]{2,1,0:T(8,128)S(1)}, f32[29,8,128]{2,1,0:T(8,128)S(1)}, u32[]{:S(2)}, u32[]{:S(2)}) collective-permute-start(f32[29,8,128]{2,1,0:T(8,128)S(1)} %get-tuple-element.31), channel_id=1, source_target_pairs={{1,2},{2,1},{3,4},{4,3},{5,6},{6,5},{7,8},{8,7},{9,10},{10,9},{11,... | collective-permute-start | bytes 356360 | tf_op jit(solution)/shard_map/ppermute | solution.py:24
  22.0 13.8 %collective-permute-start.2 = (f32[6,8,128]{2,1,0:T(8,128)S(1)}, f32[6,8,128]{2,1,0:T(8,128)S(1)}, u32[]{:S(2)}, u32[]{:S(2)}) collective-permute-start(f32[6,8,128]{2,1,0:T(8,128)S(1)} %get-tuple-element.36), channel_id=1, source_target_pairs={{0,16},{16,0},{32,48},{48,32},{1,17},{17,1},{33,49},{49,33},{2,18}... | collective-permute-start | bytes 73736 | tf_op jit(solution)/shard_map/ppermute | solution.py:24
  23.9 12.4 %collective-permute-start.3 = (f32[6,8,128]{2,1,0:T(8,128)S(1)}, f32[6,8,128]{2,1,0:T(8,128)S(1)}, u32[]{:S(2)}, u32[]{:S(2)}) collective-permute-start(f32[6,8,128]{2,1,0:T(8,128)S(1)} %get-tuple-element.37), channel_id=1, source_target_pairs={{16,32},{32,16},{17,33},{33,17},{18,34},{34,18},{19,35},{35,19},{2... | collective-permute-start | bytes 73736 | tf_op jit(solution)/shard_map/ppermute | solution.py:24
  62.8 10.8 %collective-permute-start.6 = (f32[4,8,128]{2,1,0:T(8,128)S(1)}, f32[4,8,128]{2,1,0:T(8,128)S(1)}, u32[]{:S(2)}, u32[]{:S(2)}) collective-permute-start(f32[4,8,128]{2,1,0:T(8,128)S(1)} %get-tuple-element.49), channel_id=1, source_target_pairs={{0,16},{16,0},{32,48},{48,32},{1,17},{17,1},{33,49},{49,33},{2,18}... | collective-permute-start | bytes 49160 | tf_op jit(solution)/shard_map/ppermute | solution.py:24
  64.7 9.6 %collective-permute-start.7 = (f32[4,8,128]{2,1,0:T(8,128)S(1)}, f32[4,8,128]{2,1,0:T(8,128)S(1)}, u32[]{:S(2)}, u32[]{:S(2)}) collective-permute-start(f32[4,8,128]{2,1,0:T(8,128)S(1)} %get-tuple-element.50), channel_id=1, source_target_pairs={{16,32},{32,16},{17,33},{33,17},{18,34},{34,18},{19,35},{35,19},{2... | collective-permute-start | bytes 49160 | tf_op jit(solution)/shard_map/ppermute | solution.py:24
